TPU v7x, 512 devices: a whole 4x8x8 slice. The times are simulated.
512 devices in a mesh: seq: 64 (over z, x, core), head: 8 (over y).
Axes of the slice: x: 4, y: 8, z: 8, core: 2. Of those that a mesh axis runs over, the one named last changes fastest.
Arguments:
- queries: float32 [24576, 4096], P('seq', 'head'), may hold values from -1.75 to 1.75
- key_vectors: float32 [24576, 4096], P('seq', 'head'), may hold values from -1.75 to 1.75
- value_vectors: float32 [24576, 4096], P('seq', 'head'), may hold values from -6 to 6
- out_grad: float32 [24576, 4096], P('seq', 'head'), may hold values from -6 to 6
- norm_gain: float32 [4096], P('head'), may hold values from 0.5 to 1.5
- decay_rates: float32 [32], P('head'), may hold values from 4.0690105e-07 to 0.05
- segment_ids: int32 [24576], P('seq'), may hold values from 0 to 5, never falling along the last dimension, each value on 1 to 8192 neighbouring positions
Outputs:
- query_grad: bfloat16 [24576, 4096], P('seq', 'head')
- key_grad: bfloat16 [24576, 4096], P('seq', 'head')
- value_grad: bfloat16 [24576, 4096], P('seq', 'head')
- gain_grad: float32 [4096], P('head')
Inputs may be any that keep to these rules, and one draw needn't show every extreme that they name: `segment_ids`: segment numbers never fall along the tokens; each of the 6 segments is one run of 1 to 8192 tokens, and one has exactly 8192.
All inputs are finite; a program needn't handle non-finite values.
Results may differ from a plain program's by a relative error of at most 0.001.
Values sent between devices are 32-bit elements; how exact they have to be, the bound alone decides.
No kernel may reach another device: no remote copies, remote signals or barrier semaphores. Data moves between devices by JAX's collectives and lax.ppermute only.
A program may use at most 128 MiB of HBM per device.

v0:
```python
import functools
import jax
import jax.numpy as jnp
from jax import lax
from jax.experimental import pallas as pl
from jax.experimental.pallas import tpu as pltpu
from jax.sharding import PartitionSpec as P

F32 = jnp.float32
BF16 = jnp.bfloat16
D = 128
L = 384
NH = 4
G = 16
NG = 4
PER = 4
CH = 32
PR = CH + 8
EPS = 1e-06
GROUPS = [[G * z + i for i in range(G)] for z in range(NG)]
COLUMNS = [[G * z + i for z in range(NG)] for i in range(G)]
SMEM = pltpu.SMEM
VMEM = 12 << 20


def split(x):
    hi = x.astype(BF16)
    return hi, (x - hi.astype(F32)).astype(BF16)


def dot3(a, b, ca, cb):
    dims = (((ca,), (cb,)), ((), ()))
    dg = functools.partial(lax.dot_general, dimension_numbers=dims, preferred_element_type=F32)
    return dg(a[0], b[0]) + (dg(a[0], b[1]) + dg(a[1], b[0]))


def first_at_least(seg_ref, value):
    lo = jnp.int32(0)
    size = jnp.int32(0)
    for step in (256, 128, 64, 32, 16, 8, 4, 2, 1):
        probe = lo + step
        inside = probe <= L
        below = seg_ref[jnp.minimum(probe, L) - 1] < value
        lo = jnp.where(inside & below, probe, lo)
    return lo + size


def rows_iota(n=L):
    return lax.broadcasted_iota(jnp.int32, (n, D), 0)


def seg_of(places, bounds):
    s = jnp.zeros(places.shape, jnp.int32)
    for b in bounds:
        s = s + (places >= b).astype(jnp.int32)
    return s


def notes(first, last, rate, gain=0.0):
    row = lax.broadcasted_iota(jnp.int32, (8, D), 0)
    rest = jnp.where(row == 2, rate, jnp.where(row == 3, gain, 0.0))
    return jnp.where(row == 0, first, jnp.where(row == 1, last, rest))


def put_state(out_ref, state, note):
    for t in range(PER):
        out_ref[t * PR : t * PR + CH, :] = state[t * CH : (t + 1) * CH]
        out_ref[t * PR + CH : (t + 1) * PR, :] = note


def k_state(seg_ref, rate_ref, k_ref, v_ref, out_ref, start_ref):
    h = pl.program_id(0)
    rate = rate_ref[h]
    first, last = seg_ref[0], seg_ref[L - 1]

    @pl.when(h == 0)
    def _():
        start_ref[0] = first_at_least(seg_ref, last)

    i = rows_iota()
    b = jnp.where(i >= start_ref[0], jnp.exp(-rate * (L - 1 - i).astype(F32)), 0.0)
    u = dot3(split(k_ref[...] * b), split(v_ref[...]), 0, 0)
    put_state(out_ref, u, notes(first.astype(F32), last.astype(F32), rate))


def weights(rate, bounds, rb):
    n = (rb + 1) * D
    i = lax.broadcasted_iota(jnp.int32, (D, n), 0) + rb * D
    j = lax.broadcasted_iota(jnp.int32, (D, n), 1)
    si = seg_of(lax.broadcasted_iota(jnp.int32, (D, 1), 0) + rb * D, bounds)
    sj = seg_of(lax.broadcasted_iota(jnp.int32, (1, n), 1), bounds)
    dist = jnp.maximum(i - j, 0).astype(F32)
    return jnp.where((i >= j) & (si == sj), jnp.exp(-rate * dist), 0.0)


def k_bounds(seg_ref, rate_ref, q_ref, k_ref, v_ref, o_ref, bnd_ref):
    @pl.when(pl.program_id(0) == 0)
    def _():
        for t in range(1, 6):
            bnd_ref[t - 1] = first_at_least(seg_ref, t)
        bnd_ref[5] = first_at_least(seg_ref, seg_ref[0] + 1)
        bnd_ref[6] = first_at_least(seg_ref, seg_ref[L - 1])
        bnd_ref[7] = 0

    k_local(0, bnd_ref, rate_ref, q_ref, k_ref, v_ref, o_ref)


def k_local(start, bnd_ref, rate_ref, q_ref, k_ref, v_ref, *rest):
    o_ref = rest[-1]
    h = pl.program_id(0) + start
    bounds = [bnd_ref[t] for t in range(5)]
    rate = rate_ref[h]
    qs, ks, vs = split(q_ref[...]), split(k_ref[...]), split(v_ref[...])
    for rb in range(3):
        n = (rb + 1) * D
        qr = [x[rb * D : n] for x in qs]
        kc = [x[:n] for x in ks]
        vc = [x[:n] for x in vs]
        a = dot3(qr, kc, 1, 1) * weights(rate, bounds, rb)
        o_ref[rb * D : n, :] = dot3(split(a), vc, 1, 0)


def chain(recv_ref, state, reverse, take):
    rate = recv_ref[CH + 2 : CH + 3, :]
    lam = jnp.exp(-rate * float(L))
    order = range(G - 1, -1, -1) if reverse else range(G)
    prev = None
    for i in order:
        base = i * PR
        enter = recv_ref[base + CH + (1 if reverse else 0) : base + CH + (2 if reverse else 1), :]
        leave = recv_ref[base + CH + (0 if reverse else 1) : base + CH + (1 if reverse else 2), :]
        if prev is not None:
            state = jnp.where(prev == enter, 1.0, 0.0) * state
        take(i, state)
        here = recv_ref[base : base + CH, :]
        if state is None:
            state = here
        else:
            state = here + jnp.where(enter == leave, lam, 0.0) * state
        prev = leave
    return state


def k_total(recv_ref, *rest, reverse):
    t_ref = rest[-1]
    t_ref[0:CH, :] = chain(recv_ref, jnp.zeros((CH, D), F32), reverse, lambda i, s: None)
    note = recv_ref[CH:PR, :]
    row = lax.broadcasted_iota(jnp.int32, (8, D), 0)
    out = jnp.where(row == 1, recv_ref[(G - 1) * PR + CH : G * PR, :], note)
    if reverse:
        for i in range(1, G):
            note = note + recv_ref[i * PR + CH : (i + 1) * PR, :]
        out = jnp.where(row == 3, note, out)
    t_ref[CH:PR, :] = out
    for t in range(1, NG):
        t_ref[t * PR : (t + 1) * PR, :] = t_ref[0:PR, :]


def k_carry(recv_ref, t_ref, *rest, reverse):
    out_ref = rest[-1]
    mine = lax.div(lax.axis_index("seq"), G)
    rate = recv_ref[CH + 2 : CH + 3, :]
    edge = G - 1 if reverse else 0
    row = edge * PR + CH + (1 if reverse else 0)
    enter = recv_ref[row : row + 1, :]
    state = jnp.zeros((CH, D), F32)
    gain = jnp.zeros((8, D), F32)
    for g in range(NG):
        base = g * PR
        leave = base + CH + (0 if reverse else 1)
        gap = (g - 1 - mine) if reverse else (mine - 1 - g)
        same = (t_ref[leave : leave + 1, :] == enter) & (gap >= 0)
        power = jnp.maximum(gap, 0).astype(F32) * float(L * G)
        state = state + jnp.where(same, jnp.exp(-rate * power), 0.0) * t_ref[base : base + CH, :]
        gain = gain + t_ref[base + CH : base + PR, :]
    rows = PR if reverse else CH

    def take(i, s):
        out_ref[i * rows : i * rows + CH, :] = s
        if reverse:
            out_ref[i * rows + CH : i * rows + PR, :] = gain

    chain(recv_ref, state, reverse, take)


def k_norm(bnd_ref, rate_ref, q_ref, c_ref, ol_ref, og_ref, gain_ref, o_ref, red_ref, sq, pr):
    h = pl.program_id(0)
    rate = rate_ref[h]
    i = rows_iota()
    a = jnp.where(i < bnd_ref[5], jnp.exp(-rate * (i + 1).astype(F32)), 0.0)
    o = ol_ref[...] + a * dot3(split(q_ref[...]), split(c_ref[...]), 1, 0)
    o_ref[...] = o
    g = og_ref[...] * gain_ref[...].reshape(1, D)

    @pl.when(h == 0)
    def _():
        sq[...] = o * o
        pr[...] = g * o

    @pl.when(h > 0)
    def _():
        sq[...] += o * o
        pr[...] += g * o

    @pl.when(h == NH - 1)
    def _():
        ones = jnp.ones((8, D), BF16)
        dims = (((1,), (1,)), ((), ()))
        dg = functools.partial(lax.dot_general, dimension_numbers=dims, preferred_element_type=F32)
        rows = []
        for ref in (sq, pr):
            hi, lo = split(ref[...])
            both = dg(ones, hi) + dg(ones, lo)
            rows += [both[0:1, t * D : (t + 1) * D] for t in range(3)]
        tile = jnp.concatenate(rows + [jnp.zeros((2, D), F32)], axis=0)
        for t in range(8):
            red_ref[8 * t : 8 * t + 8, :] = tile


def k_grad(
    seg_ref, bnd_ref, rate_ref, red_ref, og_ref, o_ref, q_ref, gain_ref,
    do_ref, out_ref, rcol, ccol,
):
    h = pl.program_id(0)
    rate = rate_ref[h]

    @pl.when(h == 0)
    def _():
        tot = red_ref[0:8, :]
        for t in range(1, 8):
            tot = tot + red_ref[8 * t : 8 * t + 8, :]
        inv = lax.rsqrt(tot[0:3] / 4096.0 + EPS)
        coef = inv * inv * inv * (tot[3:6] / 4096.0)
        for t in range(3):
            rcol[t * D : (t + 1) * D, :] = jnp.broadcast_to(inv[t : t + 1], (D, D)).T
            ccol[t * D : (t + 1) * D, :] = jnp.broadcast_to(coef[t : t + 1], (D, D)).T

    og = og_ref[...]
    o = o_ref[...]
    r = rcol[...]
    do = r * (og * gain_ref[...].reshape(1, D)) - ccol[...] * o
    do_ref[...] = do
    i = rows_iota()
    e = jnp.where(i < bnd_ref[5], jnp.exp(-rate * i.astype(F32)), 0.0)
    v = dot3(split(q_ref[...] * e), split(do), 0, 0)
    part = jnp.sum(og * o * r, axis=0, keepdims=True)
    put_state(out_ref, v, notes(seg_ref[0].astype(F32), seg_ref[L - 1].astype(F32), rate, part))


def k_pgrad(start, bnd_ref, rate_ref, q_ref, k_ref, v_ref, do_ref, c_ref, *rest):
    dq_ref, dk_ref = rest[2:4] if start else rest[:2]
    h = pl.program_id(0) + start
    if not start:
        rest[2][...] = jnp.zeros((8, D), F32)
    rate = rate_ref[h]
    bounds = [bnd_ref[t] for t in range(5)]
    qs, ks, vs, ds = [split(x[...]) for x in (q_ref, k_ref, v_ref, do_ref)]
    cs = split(c_ref[...])
    for rb in range(3):
        n = (rb + 1) * D
        rows = slice(rb * D, n)
        dr = [x[rows] for x in ds]
        p = split(dot3(dr, [x[:n] for x in vs], 1, 1) * weights(rate, bounds, rb))
        i = rows_iota(D) + rb * D
        a = jnp.where(i < bnd_ref[5], jnp.exp(-rate * (i + 1).astype(F32)), 0.0)
        dq = dot3(p, [x[:n] for x in ks], 1, 0) + a * dot3(dr, cs, 1, 1)
        dq_ref[rows, :] = dq.astype(BF16)
        part = dot3(p, [x[rows] for x in qs], 0, 0)
        if rb == 0:
            dk_ref[0:n, :] = part
        else:
            dk_ref[0 : n - D, :] += part[: n - D]
            dk_ref[rows, :] = part[n - D :]


def k_vgrad(bnd_ref, rate_ref, q_ref, k_ref, do_ref, dv_ref):
    h = pl.program_id(0)
    rate = rate_ref[h]
    bounds = [bnd_ref[t] for t in range(5)]
    qs, ks, ds = [split(x[...]) for x in (q_ref, k_ref, do_ref)]
    for rb in range(3):
        n = (rb + 1) * D
        rows = slice(rb * D, n)
        s = dot3([x[rows] for x in qs], [x[:n] for x in ks], 1, 1)
        a = split(s * weights(rate, bounds, rb))
        part = dot3(a, [x[rows] for x in ds], 0, 0)
        if rb == 0:
            dv_ref[0:n, :] = part
        else:
            dv_ref[0 : n - D, :] += part[: n - D]
            dv_ref[rows, :] = part[n - D :]


def k_final(bnd_ref, rate_ref, k_ref, v_ref, st_ref, dkl_ref, dvl_ref, dk_ref, dv_ref, gg_ref):
    h = pl.program_id(0)
    rate = rate_ref[h]
    i = rows_iota()
    c = jnp.where(i >= bnd_ref[6], jnp.exp(-rate * (L - i).astype(F32)), 0.0)
    state = jnp.concatenate([st_ref[t * PR : t * PR + CH, :] for t in range(PER)], axis=0)
    ss = split(state)
    dk_ref[...] = (dkl_ref[...] + c * dot3(split(v_ref[...]), ss, 1, 1)).astype(BF16)
    dv_ref[...] = (dvl_ref[...] + c * dot3(split(k_ref[...]), ss, 1, 0)).astype(BF16)
    gg_ref[...] = st_ref[CH + 3, :]


def head_block(start=0):
    return pl.BlockSpec((L, D), lambda h: (0, h + start))


def rows_block(n, start=0):
    return pl.BlockSpec((n, D), lambda h: (h + start, 0))


def gain_block():
    return pl.BlockSpec((D,), lambda h: (h,))


def whole(*shape):
    return pl.BlockSpec(shape, lambda h: (0,) * len(shape))


def scalars():
    return pl.BlockSpec(memory_space=SMEM)


def sds(shape, dtype=F32):
    return jax.ShapeDtypeStruct(shape, dtype)


def far(*arrays):
    return [pltpu.with_memory_space_constraint(x, pltpu.HBM) for x in arrays]


def near(*arrays):
    return [pltpu.with_memory_space_constraint(x, pltpu.VMEM) for x in arrays]


def idle():
    return pl.BlockSpec(memory_space=pl.ANY)


def heads_call(kernel, in_specs, out_specs, out_shape, flops, scratch=(), name=None, heads=NH, aliases={}):
    return pl.pallas_call(
        kernel,
        grid=(heads,),
        input_output_aliases=aliases,
        in_specs=in_specs,
        out_specs=out_specs,
        out_shape=out_shape,
        scratch_shapes=list(scratch),
        compiler_params=pltpu.CompilerParams(
            dimension_semantics=("arbitrary",), vmem_limit_bytes=VMEM
        ),
        cost_estimate=pl.CostEstimate(flops=flops, transcendentals=0, bytes_accessed=3 << 20),
        name=name,
    )


def small_call(kernel, n_in, n_idle, out_shape, name):
    vm = pl.BlockSpec(memory_space=pltpu.VMEM)
    return pl.pallas_call(
        kernel,
        in_specs=[vm] * n_in + [idle()] * n_idle,
        out_specs=vm,
        out_shape=out_shape,
        compiler_params=pltpu.CompilerParams(vmem_limit_bytes=VMEM),
        cost_estimate=pl.CostEstimate(flops=1 << 20, transcendentals=0, bytes_accessed=1 << 19),
        name=name,
    )


def exchange(x, axis="seq", groups=GROUPS):
    return lax.all_to_all(x, axis, 0, 0, tiled=True, axis_index_groups=groups)


def scan_in(payload, reverse, order=()):
    recv = exchange(payload)
    total = small_call(
        functools.partial(k_total, reverse=reverse), 1, len(order), sds((NG * PR, D)), "total"
    )(recv, *order)
    return recv, exchange(total, "seq", COLUMNS)


def scan_out(recv, totals, reverse, order=()):
    rows = PR if reverse else CH
    back = small_call(
        functools.partial(k_carry, reverse=reverse), 2, len(order), sds((G * rows, D)), "carry"
    )(recv, totals, *order)
    return exchange(back)


def body(queries, key_vectors, value_vectors, out_grad, norm_gain, decay_rates, segment_ids):
    hb, sc = head_block(), scalars()
    big = 9 * 2 * L * L * D * NH
    flat = pltpu.VMEM((L, NH * D), F32)
    q, k, v, rates, segs = far(queries, key_vectors, value_vectors, decay_rates, segment_ids)
    payload = heads_call(
        k_state,
        [sc, sc, hb, hb],
        rows_block(PER * PR),
        sds((G * PR, D)),
        big // 6,
        [pltpu.SMEM((1,), jnp.int32)],
        name="state",
    )(segs, rates, k, v)
    half = NH // 2
    late = head_block(half)
    local_out, bnd = heads_call(
        k_bounds,
        [sc, sc, hb, hb, hb],
        [hb, sc],
        [flat, pltpu.HBM((8,), jnp.int32)],
        big // 2,
        name="local",
        heads=half,
    )(segs, rates, q, k, v)
    (bnd,) = far(bnd)
    recv, totals = scan_in(payload, False, (bnd,))
    carry = scan_out(recv, totals, False)
    local_out = heads_call(
        functools.partial(k_local, half),
        [sc, sc, late, late, late, idle()],
        late,
        flat,
        big // 2,
        name="local2",
        heads=half,
        aliases={5: 0},
    )(bnd, rates, q, k, v, *near(local_out))
    out, red = heads_call(
        k_norm,
        [sc, sc, hb, rows_block(D), hb, hb, gain_block()],
        [hb, whole(64, D)],
        [flat, sds((64, D))],
        big // 6,
        [pltpu.VMEM((L, D), F32)] * 2,
        name="norm",
    )(bnd, rates, queries, carry, *near(local_out), out_grad, *far(norm_gain))
    sums = exchange(red, "head", None)
    grad_out, payload = heads_call(
        k_grad,
        [sc, sc, sc, whole(64, D), hb, hb, hb, gain_block()],
        [hb, rows_block(PER * PR)],
        [flat, pltpu.HBM((G * PR, D), F32)],
        big // 6,
        [pltpu.VMEM((L, D), F32)] * 2,
        name="grad",
    )(segs, bnd, rates, sums, out_grad, *near(out), queries, *far(norm_gain))
    (grad_out,) = near(grad_out)
    dv_local = heads_call(
        k_vgrad, [sc, sc, hb, hb, hb], hb, flat, big // 2, name="vgrad"
    )(bnd, rates, q, k, grad_out)
    outs = [pltpu.HBM((L, NH * D), BF16), pltpu.HBM((L, NH * D), F32)]
    dq, dk_local, mark = heads_call(
        functools.partial(k_pgrad, 0),
        [sc, sc, hb, hb, hb, hb, rows_block(D)],
        [hb, hb, whole(8, D)],
        outs + [sds((8, D))],
        big // 2,
        name="pgrad",
        heads=half,
    )(bnd, rates, q, k, v, grad_out, carry)
    recv, totals = scan_in(payload, True, (dv_local,))
    back = scan_out(recv, totals, True, (mark,))
    dq, dk_local = heads_call(
        functools.partial(k_pgrad, half),
        [sc, sc, late, late, late, late, rows_block(D, half), idle(), idle()],
        [late, late],
        outs,
        big // 2,
        name="pgrad2",
        heads=half,
        aliases={7: 0, 8: 1},
    )(bnd, rates, q, k, v, grad_out, carry, *far(dq, dk_local))
    dk, dv, gain_grad = heads_call(
        k_final,
        [sc, sc, hb, hb, rows_block(PER * PR), hb, hb],
        [hb, hb, gain_block()],
        [sds((L, NH * D), BF16), sds((L, NH * D), BF16), sds((NH * D,))],
        big // 6,
        name="final",
    )(bnd, rates, key_vectors, value_vectors, back, *far(dk_local), *near(dv_local))
    return dq, dk, dv, gain_grad


def solution(mesh):
    return jax.shard_map(
        body,
        mesh=mesh,
        in_specs=(
            P("seq", "head"),
            P("seq", "head"),
            P("seq", "head"),
            P("seq", "head"),
            P("head"),
            P("head"),
            P("seq"),
        ),
        out_specs=(P("seq", "head"), P("seq", "head"), P("seq", "head"), P("head")),
        check_vma=False,
    )
```

profile of v0, /device:TPU:1, one launch (start us, length us, event | category | flops | bytes accessed | tf_op | source)
XLA Modules:
  0.0 113.8 jit_solution(2020506418732088964)
XLA Ops:
  0.6 4.1 %state.1 = f32[640,128]{1,0:T(8,128)} custom-call(s32[384]{0:T(512)} %seg_ref.5, f32[4]{0:T(128)} %rate_ref.17, f32[384,512]{1,0:T(8,128)} %k_ref.13, f32[384,512]{1,0:T(8,128)} %v_ref.11), custom_call_target="tpu_custom_call" | custom-call | flops 226492416 | bytes 3145728 | tf_op jit(solution)/shard_map/state/pallas_call | solution.py:397
  4.8 10.2 %all-to-all-start = ((f32[16,40,128]{2,1,0:T(8,128)}), f32[16,40,128]{2,1,0:T(8,128)S(1)}, u32[]{:S(2)}, u32[]{:S(2)}) async-start(f32[16,40,128]{2,1,0:T(8,128)} %bitcast), calls=%async_computation | async-start | bytes 655360 | tf_op jit(solution)/shard_map/all_to_all | solution.py:373
  14.9 3.9 %local.1 = (f32[384,512]{1,0:T(8,128)S(1)}, s32[8]{0:T(128)}) custom-call(s32[384]{0:T(512)} %seg_ref.5, f32[4]{0:T(128)} %rate_ref.17, f32[384,512]{1,0:T(8,128)} %q_ref.13, f32[384,512]{1,0:T(8,128)} %k_ref.13, f32[384,512]{1,0:T(8,128)} %v_ref.11), custom_call_target="tpu_custom_call" | custom-call | flops 679477248 | bytes 3145728 | tf_op jit(solution)/shard_map/local/pallas_call | solution.py:408
  18.9 3.8 %all-to-all-done = f32[16,40,128]{2,1,0:T(8,128)S(1)} async-done(((f32[16,40,128]{2,1,0:T(8,128)}), f32[16,40,128]{2,1,0:T(8,128)S(1)}, u32[]{:S(2)}, u32[]{:S(2)}) %all-to-all-start) | async-done | bytes 327712 | tf_op jit(solution)/shard_map/all_to_all | solution.py:373
  22.7 0.1 total.2
  22.8 13.4 %all_to_all.77 = f32[4,40,128]{2,1,0:T(8,128)S(1)} all-to-all(f32[4,40,128]{2,1,0:T(8,128)S(1)} %bitcast.21), channel_id=1, replica_groups={{0,128,256,384},{8,136,264,392},{16,144,272,400},{24,152,280,408},{32,1..., dimensions={0} | all-to-all | bytes 163840 | tf_op jit(solution)/shard_map/all_to_all | solution.py:373
  36.1 0.8 carry.2
  36.9 6.0 %all-to-all-start.2 = ((f32[16,32,128]{2,1,0:T(8,128)}), f32[16,32,128]{2,1,0:T(8,128)S(1)}, u32[]{:S(2)}, u32[]{:S(2)}) async-start(f32[16,32,128]{2,1,0:T(8,128)} %bitcast.4), calls=%async_computation.2 | async-start | bytes 524288 | tf_op jit(solution)/shard_map/all_to_all | solution.py:373
  42.9 0.0 copy-start.1
  42.9 0.0 copy-start.3
  42.9 3.3 %local2.1.ol_ref = f32[384,512]{1,0:T(8,128)S(1)} custom-call(s32[8]{0:T(128)} %get-tuple-element.18.rest_0_.bnd_ref, f32[4]{0:T(128)} %rate_ref.17, f32[384,512]{1,0:T(8,128)} %q_ref.13, f32[384,512]{1,0:T(8,128)} %k_ref.13, f32[384,512]{1,0:T(8,128)} %v_ref.11, f32[384,512]{1,0:T(8,128)S(1)} %get-tuple-element.19.rest_0_), custom_call_target="tpu_custom_call", output_to_operand_aliasing={{}: (5, {})} | custom-call | flops 679477248 | bytes 3145728 | tf_op jit(solution)/shard_map/local2/pallas_call | solution.py:420
  46.2 4.0 %all-to-all-done.2 = f32[16,32,128]{2,1,0:T(8,128)S(1)} async-done(((f32[16,32,128]{2,1,0:T(8,128)}), f32[16,32,128]{2,1,0:T(8,128)S(1)}, u32[]{:S(2)}, u32[]{:S(2)}) %all-to-all-start.2) | async-done | bytes 262176 | tf_op jit(solution)/shard_map/all_to_all | solution.py:373
  50.2 0.0 copy-done.1
  50.2 0.0 copy-done.3
  50.2 2.8 %norm.1 = (f32[384,512]{1,0:T(8,128)S(1)}, f32[64,128]{1,0:T(8,128)S(1)}) custom-call(s32[8]{0:T(128)} %get-tuple-element.18.rest_0_.bnd_ref, f32[4]{0:T(128)} %rate_ref.17, f32[384,512]{1,0:T(8,128)S(1)} %copy-done.1, f32[512,128]{1,0:T(8,128)S(1)} %bitcast.14, f32[384,512]{1,0:T(8,128)S(1)} %local2.1.ol_ref, f32[384,512]{1,0:T(8,128)S(1)} %copy-done.3, ...), custom_call_target="tpu_custom_call" | custom-call | flops 226492416 | bytes 3145728 | tf_op jit(solution)/shard_map/norm/pallas_call | solution.py:430
  53.0 13.5 %all_to_all.78 = f32[8,8,128]{2,1,0:T(8,128)S(1)} all-to-all(f32[8,8,128]{2,1,0:T(8,128)S(1)} %bitcast.25), channel_id=1, replica_groups=mesh['seq'=64,'head'=8] {'head'}, dimensions={0} | all-to-all | bytes 65536 | tf_op jit(solution)/shard_map/all_to_all | solution.py:373
  66.5 3.7 %grad.1 = (f32[384,512]{1,0:T(8,128)S(1)}, f32[640,128]{1,0:T(8,128)}) custom-call(s32[384]{0:T(512)} %seg_ref.5, s32[8]{0:T(128)} %get-tuple-element.18.rest_0_.bnd_ref, f32[4]{0:T(128)} %rate_ref.17, f32[64,128]{1,0:T(8,128)S(1)} %bitcast.24, f32[384,512]{1,0:T(8,128)S(1)} %copy-done.3, f32[384,512]{1,0:T(8,128)S(1)} %get-tuple-element.21.o_ref, ...), custom_call_target="tpu_custom_call" | custom-call | flops 226492416 | bytes 3145728 | tf_op jit(solution)/shard_map/grad/pallas_call | solution.py:440
  70.2 5.7 %all-to-all-start.4 = ((f32[16,40,128]{2,1,0:T(8,128)}), f32[16,40,128]{2,1,0:T(8,128)S(1)}, u32[]{:S(2)}, u32[]{:S(2)}) async-start(f32[16,40,128]{2,1,0:T(8,128)} %bitcast.26), calls=%async_computation.4 | async-start | bytes 655360 | tf_op jit(solution)/shard_map/all_to_all | solution.py:373
  75.9 5.2 %vgrad.1.rest_0_.dvl_ref = f32[384,512]{1,0:T(8,128)S(1)} custom-call(s32[8]{0:T(128)} %get-tuple-element.18.rest_0_.bnd_ref, f32[4]{0:T(128)} %rate_ref.17, f32[384,512]{1,0:T(8,128)} %q_ref.13, f32[384,512]{1,0:T(8,128)} %k_ref.13, f32[384,512]{1,0:T(8,128)S(1)} %get-tuple-element.22.do_ref), custom_call_target="tpu_custom_call" | custom-call | flops 679477248 | bytes 3145728 | tf_op jit(solution)/shard_map/vgrad/pallas_call | solution.py:450
  81.0 2.6 %all-to-all-done.4 = f32[16,40,128]{2,1,0:T(8,128)S(1)} async-done(((f32[16,40,128]{2,1,0:T(8,128)}), f32[16,40,128]{2,1,0:T(8,128)S(1)}, u32[]{:S(2)}, u32[]{:S(2)}) %all-to-all-start.4) | async-done | bytes 327712 | tf_op jit(solution)/shard_map/all_to_all | solution.py:373
  83.6 0.7 total.3
  84.3 3.3 %all-to-all-start.5 = ((f32[4,40,128]{2,1,0:T(8,128)}), f32[4,40,128]{2,1,0:T(8,128)S(1)}, u32[]{:S(2)}, u32[]{:S(2)}) async-start(f32[4,40,128]{2,1,0:T(8,128)} %bitcast.10), calls=%async_computation.5 | async-start | bytes 163840 | tf_op jit(solution)/shard_map/all_to_all | solution.py:373
  87.6 4.6 %pgrad.1 = (bf16[384,512]{1,0:T(8,128)(2,1)}, f32[384,512]{1,0:T(8,128)}, f32[8,128]{1,0:T(8,128)S(1)}) custom-call(s32[8]{0:T(128)} %get-tuple-element.18.rest_0_.bnd_ref, f32[4]{0:T(128)} %rate_ref.17, f32[384,512]{1,0:T(8,128)} %q_ref.13, f32[384,512]{1,0:T(8,128)} %k_ref.13, f32[384,512]{1,0:T(8,128)} %v_ref.11, ...), custom_call_target="tpu_custom_call" | custom-call | flops 679477248 | bytes 3145728 | tf_op jit(solution)/shard_map/pgrad/pallas_call | solution.py:454
  92.2 2.4 %all-to-all-done.5 = f32[4,40,128]{2,1,0:T(8,128)S(1)} async-done(((f32[4,40,128]{2,1,0:T(8,128)}), f32[4,40,128]{2,1,0:T(8,128)S(1)}, u32[]{:S(2)}, u32[]{:S(2)}) %all-to-all-start.5) | async-done | bytes 81952 | tf_op jit(solution)/shard_map/all_to_all | solution.py:373
  94.5 0.8 carry.3
  95.4 6.5 %all-to-all-start.6 = ((f32[16,40,128]{2,1,0:T(8,128)}), f32[16,40,128]{2,1,0:T(8,128)}, u32[]{:S(2)}, u32[]{:S(2)}) async-start(f32[16,40,128]{2,1,0:T(8,128)} %bitcast.12), calls=%async_computation.6 | async-start | bytes 655360 | tf_op jit(solution)/shard_map/all_to_all | solution.py:373
  101.8 0.0 copy-start
  101.8 0.0 copy-start.2
  101.8 4.7 %pgrad2.1 = (bf16[384,512]{1,0:T(8,128)(2,1)}, f32[384,512]{1,0:T(8,128)}) custom-call(s32[8]{0:T(128)} %get-tuple-element.18.rest_0_.bnd_ref, f32[4]{0:T(128)} %rate_ref.17, f32[384,512]{1,0:T(8,128)} %q_ref.13, f32[384,512]{1,0:T(8,128)} %k_ref.13, f32[384,512]{1,0:T(8,128)} %v_ref.11, ...), custom_call_target="tpu_custom_call", output_to_operand_aliasing={{0}: (7, {}), {1}: (8, {})} | custom-call | flops 679477248 | bytes 3145728 | tf_op jit(solution)/shard_map/pgrad2/pallas_call | solution.py:465
  106.5 3.2 %all-to-all-done.6 = f32[16,40,128]{2,1,0:T(8,128)} async-done(((f32[16,40,128]{2,1,0:T(8,128)}), f32[16,40,128]{2,1,0:T(8,128)}, u32[]{:S(2)}, u32[]{:S(2)}) %all-to-all-start.6) | async-done | bytes 327712 | tf_op jit(solution)/shard_map/all_to_all | solution.py:373
  109.7 0.0 copy-done
  109.7 0.0 copy-done.2
  109.7 4.1 %final.1 = (bf16[384,512]{1,0:T(8,128)(2,1)}, bf16[384,512]{1,0:T(8,128)(2,1)}, f32[512]{0:T(512)}) custom-call(s32[8]{0:T(128)} %get-tuple-element.18.rest_0_.bnd_ref, f32[4]{0:T(128)} %rate_ref.17, f32[384,512]{1,0:T(8,128)S(1)} %copy-done, f32[384,512]{1,0:T(8,128)S(1)} %copy-done.2, f32[640,128]{1,0:T(8,128)} %bitcast.13.st_ref, ...), custom_call_target="tpu_custom_call" | custom-call | flops 226492416 | bytes 3145728 | tf_op jit(solution)/shard_map/final/pallas_call | solution.py:475
Async XLA Ops:
  4.8 17.9 %all-to-all-start = ((f32[16,40,128]{2,1,0:T(8,128)}), f32[16,40,128]{2,1,0:T(8,128)S(1)}, u32[]{:S(2)}, u32[]{:S(2)}) async-start(f32[16,40,128]{2,1,0:T(8,128)} %bitcast), calls=%async_computation | async-start | bytes 655360 | tf_op jit(solution)/shard_map/all_to_all | solution.py:373
  36.9 13.3 %all-to-all-start.2 = ((f32[16,32,128]{2,1,0:T(8,128)}), f32[16,32,128]{2,1,0:T(8,128)S(1)}, u32[]{:S(2)}, u32[]{:S(2)}) async-start(f32[16,32,128]{2,1,0:T(8,128)} %bitcast.4), calls=%async_computation.2 | async-start | bytes 524288 | tf_op jit(solution)/shard_map/all_to_all | solution.py:373
  42.9 7.3 %copy-start.1 = (f32[384,512]{1,0:T(8,128)S(1)}, f32[384,512]{1,0:T(8,128)}, u32[]{:S(2)}) copy-start(f32[384,512]{1,0:T(8,128)} %q_ref.13) | copy-start | bytes 2359300
  42.9 7.3 %copy-start.3 = (f32[384,512]{1,0:T(8,128)S(1)}, f32[384,512]{1,0:T(8,128)}, u32[]{:S(2)}) copy-start(f32[384,512]{1,0:T(8,128)} %og_ref.3) | copy-start | bytes 2359300
  70.2 13.4 %all-to-all-start.4 = ((f32[16,40,128]{2,1,0:T(8,128)}), f32[16,40,128]{2,1,0:T(8,128)S(1)}, u32[]{:S(2)}, u32[]{:S(2)}) async-start(f32[16,40,128]{2,1,0:T(8,128)} %bitcast.26), calls=%async_computation.4 | async-start | bytes 655360 | tf_op jit(solution)/shard_map/all_to_all | solution.py:373
  84.3 10.2 %all-to-all-start.5 = ((f32[4,40,128]{2,1,0:T(8,128)}), f32[4,40,128]{2,1,0:T(8,128)S(1)}, u32[]{:S(2)}, u32[]{:S(2)}) async-start(f32[4,40,128]{2,1,0:T(8,128)} %bitcast.10), calls=%async_computation.5 | async-start | bytes 163840 | tf_op jit(solution)/shard_map/all_to_all | solution.py:373
  95.4 14.3 %all-to-all-start.6 = ((f32[16,40,128]{2,1,0:T(8,128)}), f32[16,40,128]{2,1,0:T(8,128)}, u32[]{:S(2)}, u32[]{:S(2)}) async-start(f32[16,40,128]{2,1,0:T(8,128)} %bitcast.12), calls=%async_computation.6 | async-start | bytes 655360 | tf_op jit(solution)/shard_map/all_to_all | solution.py:373
  101.8 7.9 %copy-start = (f32[384,512]{1,0:T(8,128)S(1)}, f32[384,512]{1,0:T(8,128)}, u32[]{:S(2)}) copy-start(f32[384,512]{1,0:T(8,128)} %k_ref.13) | copy-start | bytes 2359300
  101.8 7.8 %copy-start.2 = (f32[384,512]{1,0:T(8,128)S(1)}, f32[384,512]{1,0:T(8,128)}, u32[]{:S(2)}) copy-start(f32[384,512]{1,0:T(8,128)} %v_ref.11) | copy-start | bytes 2359300
where the time goes:
time: 115 us; the launch traced here: 114 us
  Pallas kernels  38.6 us (34%)
  starting transfers between devices  31.6 us (27%)
  blocking collectives  26.9 us (23%)
  waiting for transfers between devices  15.9 us (14%)
    all_to_all x5, starting transfers between devices, exchange(): return lax.all_to_all(x, axis, 0, 0, tiled=True, axis_index_groups=groups)  31.6 us
    all_to_all x2, blocking collectives, exchange(): return lax.all_to_all(x, axis, 0, 0, tiled=True, axis_index_groups=groups)  26.9 us
    all_to_all x5, waiting for transfers between devices, exchange(): return lax.all_to_all(x, axis, 0, 0, tiled=True, axis_index_groups=groups)  15.9 us
    pallas_call x1, Pallas kernels, body(): heads_call(k_vgrad, [sc, sc, hb, hb, hb], hb, flat, big // 2, name='vgrad')  5.15 us
    pallas_call x1, Pallas kernels, body(): heads_call(functools.partial(k_pgrad, half), [sc, sc, late, late, late, l...  4.66 us
    pallas_call x1, Pallas kernels, body(): heads_call(functools.partial(k_pgrad, 0), [sc, sc, hb, hb, hb, hb, rows_b...  4.56 us
    pallas_call x1, Pallas kernels, body(): heads_call(k_state, [sc, sc, hb, hb], rows_block(PER * PR), sds((G * PR,...  4.14 us
    pallas_call x1, Pallas kernels, body(): heads_call(k_final, [sc, sc, hb, hb, rows_block(PER * PR), hb, hb], [hb,...  4.09 us
  transfers between devices with their start and end apart: 5, of which 5 were waited for; matrix products, arithmetic and copies ran while one was open for 0% of the time, Pallas kernels for 19%

commit v1 on v0

v1 whole, which is shorter than its diff:
```python
import functools
import jax
import jax.numpy as jnp
from jax import lax
from jax.experimental import pallas as pl
from jax.experimental.pallas import tpu as pltpu
from jax.sharding import PartitionSpec as P

F32 = jnp.float32
BF16 = jnp.bfloat16
D = 128
L = 384
NH = 4
G = 16
NG = 4
PER = 4
CH = 32
PR = CH + 8
EPS = 1e-06
GROUPS = [[G * z + i for i in range(G)] for z in range(NG)]
COLUMNS = [[G * z + i for z in range(NG)] for i in range(G)]
SMEM = pltpu.SMEM
VMEM = 12 << 20


def split(x):
    hi = x.astype(BF16)
    return hi, (x - hi.astype(F32)).astype(BF16)


def dot3(a, b, ca, cb):
    dims = (((ca,), (cb,)), ((), ()))
    dg = functools.partial(lax.dot_general, dimension_numbers=dims, preferred_element_type=F32)
    return dg(a[0], b[0]) + (dg(a[0], b[1]) + dg(a[1], b[0]))


def first_at_least(seg_ref, value):
    lo = jnp.int32(0)
    size = jnp.int32(0)
    for step in (256, 128, 64, 32, 16, 8, 4, 2, 1):
        probe = lo + step
        inside = probe <= L
        below = seg_ref[jnp.minimum(probe, L) - 1] < value
        lo = jnp.where(inside & below, probe, lo)
    return lo + size


def rows_iota(n=L):
    return lax.broadcasted_iota(jnp.int32, (n, D), 0)


def seg_of(places, bounds):
    s = jnp.zeros(places.shape, jnp.int32)
    for b in bounds:
        s = s + (places >= b).astype(jnp.int32)
    return s


def notes(first, last, rate, gain=0.0):
    row = lax.broadcasted_iota(jnp.int32, (8, D), 0)
    rest = jnp.where(row == 2, rate, jnp.where(row == 3, gain, 0.0))
    return jnp.where(row == 0, first, jnp.where(row == 1, last, rest))


def put_state(out_ref, h, state, note):
    for t in range(PER):
        base = (h * PER + t) * PR
        out_ref[base : base + CH, :] = state[t * CH : (t + 1) * CH]
        out_ref[base + CH : base + PR, :] = note


def head(h):
    return slice(h * D, (h + 1) * D)


def k_state(seg_ref, rate_ref, k_hbm, v_hbm, out_ref, k_ref, v_ref, sems):
    copies = []
    for h in range(NH):
        for t, (src, dst) in enumerate(((k_hbm, k_ref), (v_hbm, v_ref))):
            copies.append(
                pltpu.make_async_copy(src.at[:, head(h)], dst.at[:, head(h)], sems.at[2 * h + t])
            )
            copies[-1].start()
    first, last = seg_ref[0], seg_ref[L - 1]
    start = first_at_least(seg_ref, last)
    i = rows_iota()
    back = (L - 1 - i).astype(F32)
    for h in range(NH):
        rate = rate_ref[h]
        b = jnp.where(i >= start, jnp.exp(-rate * back), 0.0)
        copies[2 * h].wait()
        copies[2 * h + 1].wait()
        u = dot3(split(k_ref[:, head(h)] * b), split(v_ref[:, head(h)]), 0, 0)
        note = notes(first.astype(F32), last.astype(F32), rate)
        put_state(out_ref, h, u, note)


def weights(rate, bounds, rb):
    n = (rb + 1) * D
    i = lax.broadcasted_iota(jnp.int32, (D, n), 0) + rb * D
    j = lax.broadcasted_iota(jnp.int32, (D, n), 1)
    si = seg_of(lax.broadcasted_iota(jnp.int32, (D, 1), 0) + rb * D, bounds)
    sj = seg_of(lax.broadcasted_iota(jnp.int32, (1, n), 1), bounds)
    dist = jnp.maximum(i - j, 0).astype(F32)
    return jnp.where((i >= j) & (si == sj), jnp.exp(-rate * dist), 0.0)


def k_local(seg_ref, rate_ref, q_ref, k_ref, v_ref, gain_ref, o_ref, bnd_ref, con_ref):
    h = pl.program_id(0)

    @pl.when(h == 0)
    def _():
        for t in range(1, 6):
            bnd_ref[t - 1] = first_at_least(seg_ref, t)
        bnd_ref[5] = first_at_least(seg_ref, seg_ref[0] + 1)
        bnd_ref[6] = first_at_least(seg_ref, seg_ref[L - 1])
        bnd_ref[7] = 0
        row = lax.broadcasted_iota(jnp.int32, (8, D), 0)
        tile = jnp.zeros((8, D), F32)
        values = [rate_ref[t] for t in range(NH)]
        values += [bnd_ref[5], bnd_ref[6], seg_ref[0], seg_ref[L - 1]]
        for t, value in enumerate(values):
            tile = jnp.where(row == t, value.astype(F32), tile)
        con_ref[0:8, :] = tile
        for t in range(NH):
            con_ref[8 + t : 9 + t, :] = gain_ref[head(t)].reshape(1, D)
        con_ref[12:16, :] = jnp.zeros((4, D), F32)

    bounds = [bnd_ref[t] for t in range(5)]
    rate = rate_ref[h]
    qs, ks, vs = split(q_ref[...]), split(k_ref[...]), split(v_ref[...])
    for rb in range(3):
        n = (rb + 1) * D
        qr = [x[rb * D : n] for x in qs]
        kc = [x[:n] for x in ks]
        vc = [x[:n] for x in vs]
        a = dot3(qr, kc, 1, 1) * weights(rate, bounds, rb)
        o_ref[rb * D : n, :] = dot3(split(a), vc, 1, 0)


def chain(recv_ref, state, reverse, take):
    rate = recv_ref[CH + 2 : CH + 3, :]
    lam = jnp.exp(-rate * float(L))
    order = range(G - 1, -1, -1) if reverse else range(G)
    prev = None
    for i in order:
        base = i * PR
        enter = recv_ref[base + CH + (1 if reverse else 0) : base + CH + (2 if reverse else 1), :]
        leave = recv_ref[base + CH + (0 if reverse else 1) : base + CH + (1 if reverse else 2), :]
        if prev is not None:
            state = jnp.where(prev == enter, 1.0, 0.0) * state
        take(i, state)
        here = recv_ref[base : base + CH, :]
        if state is None:
            state = here
        else:
            state = here + jnp.where(enter == leave, lam, 0.0) * state
        prev = leave
    return state


def k_total(recv_ref, *rest, reverse):
    t_ref = rest[-1]
    t_ref[0:CH, :] = chain(recv_ref, jnp.zeros((CH, D), F32), reverse, lambda i, s: None)
    note = recv_ref[CH:PR, :]
    row = lax.broadcasted_iota(jnp.int32, (8, D), 0)
    out = jnp.where(row == 1, recv_ref[(G - 1) * PR + CH : G * PR, :], note)
    if reverse:
        for i in range(1, G):
            note = note + recv_ref[i * PR + CH : (i + 1) * PR, :]
        out = jnp.where(row == 3, note, out)
    t_ref[CH:PR, :] = out
    for t in range(1, NG):
        t_ref[t * PR : (t + 1) * PR, :] = t_ref[0:PR, :]


def k_carry(recv_ref, t_ref, *rest, reverse):
    out_ref = rest[-1]
    mine = lax.div(lax.axis_index("seq"), G)
    rate = recv_ref[CH + 2 : CH + 3, :]
    edge = G - 1 if reverse else 0
    row = edge * PR + CH + (1 if reverse else 0)
    enter = recv_ref[row : row + 1, :]
    state = jnp.zeros((CH, D), F32)
    gain = jnp.zeros((8, D), F32)
    for g in range(NG):
        base = g * PR
        leave = base + CH + (0 if reverse else 1)
        gap = (g - 1 - mine) if reverse else (mine - 1 - g)
        same = (t_ref[leave : leave + 1, :] == enter) & (gap >= 0)
        power = jnp.maximum(gap, 0).astype(F32) * float(L * G)
        state = state + jnp.where(same, jnp.exp(-rate * power), 0.0) * t_ref[base : base + CH, :]
        gain = gain + t_ref[base + CH : base + PR, :]
    rows = PR if reverse else CH

    def take(i, s):
        out_ref[i * rows : i * rows + CH, :] = s
        if reverse:
            out_ref[i * rows + CH : i * rows + PR, :] = gain

    chain(recv_ref, state, reverse, take)


def k_norm(con_ref, q_ref, c_ref, ol_ref, og_ref, o_ref, red_ref):
    i = rows_iota().astype(F32)
    ahead = i + 1.0
    inside = i < con_ref[4:5, :]
    sq = pr = None
    for h in range(NH):
        a = jnp.where(inside, jnp.exp(-con_ref[h : h + 1, :] * ahead), 0.0)
        o = ol_ref[:, head(h)] + a * dot3(split(q_ref[:, head(h)]), split(c_ref[head(h), :]), 1, 0)
        o_ref[:, head(h)] = o
        g = og_ref[:, head(h)] * con_ref[8 + h : 9 + h, :]
        sq = o * o if h == 0 else sq + o * o
        pr = g * o if h == 0 else pr + g * o
    ones = jnp.ones((8, D), BF16)
    dims = (((1,), (1,)), ((), ()))
    dg = functools.partial(lax.dot_general, dimension_numbers=dims, preferred_element_type=F32)
    rows = []
    for x in (sq, pr):
        hi, lo = split(x)
        both = dg(ones, hi) + dg(ones, lo)
        rows += [both[0:1, head(t)] for t in range(3)]
    tile = jnp.concatenate(rows + [jnp.zeros((2, D), F32)], axis=0)
    for t in range(8):
        red_ref[8 * t : 8 * t + 8, :] = tile


def k_grad(
    con_ref, red_ref, og_ref, o_ref, q_ref, do_ref, out_ref
):
    tot = red_ref[0:8, :]
    for t in range(1, 8):
        tot = tot + red_ref[8 * t : 8 * t + 8, :]
    inv = lax.rsqrt(tot[0:3] / 4096.0 + EPS)
    coef = inv * inv * inv * (tot[3:6] / 4096.0)
    cols = []
    for x in (inv, coef):
        parts = [jnp.broadcast_to(x[t : t + 1], (D, D)).T for t in range(3)]
        cols.append(jnp.concatenate(parts, axis=0))
    r, c = cols
    i = rows_iota().astype(F32)
    inside = i < con_ref[4:5, :]
    first, last = con_ref[6:7, :], con_ref[7:8, :]
    for h in range(NH):
        rate = con_ref[h : h + 1, :]
        rog = r * og_ref[:, head(h)]
        o = o_ref[:, head(h)]
        do = rog * con_ref[8 + h : 9 + h, :] - c * o
        do_ref[:, head(h)] = do
        e = jnp.where(inside, jnp.exp(-rate * i), 0.0)
        v = dot3(split(q_ref[:, head(h)] * e), split(do), 0, 0)
        part = jnp.sum(rog * o, axis=0, keepdims=True)
        put_state(out_ref, h, v, notes(first, last, rate, part))


def k_pgrad(bnd_ref, rate_ref, q_ref, k_ref, v_ref, do_ref, c_ref, dq_ref, dk_ref):
    h = pl.program_id(0)
    rate = rate_ref[h]
    bounds = [bnd_ref[t] for t in range(5)]
    qs, ks, vs, ds = [split(x[...]) for x in (q_ref, k_ref, v_ref, do_ref)]
    cs = split(c_ref[...])
    for rb in range(3):
        n = (rb + 1) * D
        rows = slice(rb * D, n)
        dr = [x[rows] for x in ds]
        p = split(dot3(dr, [x[:n] for x in vs], 1, 1) * weights(rate, bounds, rb))
        i = rows_iota(D) + rb * D
        a = jnp.where(i < bnd_ref[5], jnp.exp(-rate * (i + 1).astype(F32)), 0.0)
        dq = dot3(p, [x[:n] for x in ks], 1, 0) + a * dot3(dr, cs, 1, 1)
        dq_ref[rows, :] = dq.astype(BF16)
        part = dot3(p, [x[rows] for x in qs], 0, 0)
        if rb == 0:
            dk_ref[0:n, :] = part
        else:
            dk_ref[0 : n - D, :] += part[: n - D]
            dk_ref[rows, :] = part[n - D :]


def k_vgrad(bnd_ref, rate_ref, q_ref, k_ref, do_ref, dv_ref):
    h = pl.program_id(0)
    rate = rate_ref[h]
    bounds = [bnd_ref[t] for t in range(5)]
    qs, ks, ds = [split(x[...]) for x in (q_ref, k_ref, do_ref)]
    for rb in range(3):
        n = (rb + 1) * D
        rows = slice(rb * D, n)
        s = dot3([x[rows] for x in qs], [x[:n] for x in ks], 1, 1)
        a = split(s * weights(rate, bounds, rb))
        part = dot3(a, [x[rows] for x in ds], 0, 0)
        if rb == 0:
            dv_ref[0:n, :] = part
        else:
            dv_ref[0 : n - D, :] += part[: n - D]
            dv_ref[rows, :] = part[n - D :]


def k_final(
    con_ref, k_ref, v_ref, st_ref, dkl_hbm, dvl_ref, dk_hbm, dv_hbm, gg_ref,
    dkl_ref, dk_ref, dv_ref, sems,
):
    loads, stores = [], []
    for h in range(NH):
        loads.append(
            pltpu.make_async_copy(dkl_hbm.at[:, head(h)], dkl_ref.at[:, head(h)], sems.at[h])
        )
        loads[-1].start()
    i = rows_iota().astype(F32)
    inside = i >= con_ref[5:6, :]
    back = float(L) - i
    for h in range(NH):
        c = jnp.where(inside, jnp.exp(-con_ref[h : h + 1, :] * back), 0.0)
        bases = [(h * PER + t) * PR for t in range(PER)]
        ss = split(jnp.concatenate([st_ref[b : b + CH, :] for b in bases], axis=0))
        gg_ref[head(h)] = st_ref[bases[0] + CH + 3, :]
        for t in range(2):
            if t == 0:
                x = dvl_ref[:, head(h)] + c * dot3(split(k_ref[:, head(h)]), ss, 1, 0)
                buf, far_ref = dv_ref, dv_hbm
            else:
                loads[h].wait()
                x = dkl_ref[:, head(h)] + c * dot3(split(v_ref[:, head(h)]), ss, 1, 1)
                buf, far_ref = dk_ref, dk_hbm
            buf[:, head(h)] = x.astype(BF16)
            stores.append(
                pltpu.make_async_copy(
                    buf.at[:, head(h)], far_ref.at[:, head(h)], sems.at[NH + 2 * h + t]
                )
            )
            stores[-1].start()
    for copy in stores:
        copy.wait()


def head_block():
    return pl.BlockSpec((L, D), lambda h: (0, h))


def rows_block(n):
    return pl.BlockSpec((n, D), lambda h: (h, 0))


def whole(*shape):
    return pl.BlockSpec(shape, lambda h: (0,) * len(shape))


def scalars():
    return pl.BlockSpec(memory_space=SMEM)


def sds(shape, dtype=F32):
    return jax.ShapeDtypeStruct(shape, dtype)


def far(*arrays):
    return [pltpu.with_memory_space_constraint(x, pltpu.HBM) for x in arrays]


def near(*arrays):
    return [pltpu.with_memory_space_constraint(x, pltpu.VMEM) for x in arrays]


def idle():
    return pl.BlockSpec(memory_space=pl.ANY)


def heads_call(kernel, in_specs, out_specs, out_shape, flops, scratch=(), name=None):
    return pl.pallas_call(
        kernel,
        grid=(NH,),
        in_specs=in_specs,
        out_specs=out_specs,
        out_shape=out_shape,
        scratch_shapes=list(scratch),
        compiler_params=pltpu.CompilerParams(
            dimension_semantics=("arbitrary",), vmem_limit_bytes=VMEM
        ),
        cost_estimate=pl.CostEstimate(flops=flops, transcendentals=0, bytes_accessed=3 << 20),
        name=name,
    )


def near_block():
    return pl.BlockSpec(memory_space=pltpu.VMEM)


def one_call(kernel, in_specs, out_specs, out_shape, name, flops=1 << 20, scratch=()):
    return pl.pallas_call(
        kernel,
        in_specs=in_specs,
        out_specs=out_specs,
        out_shape=out_shape,
        scratch_shapes=list(scratch),
        compiler_params=pltpu.CompilerParams(vmem_limit_bytes=VMEM),
        cost_estimate=pl.CostEstimate(flops=flops, transcendentals=0, bytes_accessed=1 << 19),
        name=name,
    )


def small_call(kernel, n_in, n_idle, out_shape, name):
    vm = near_block()
    return one_call(kernel, [vm] * n_in + [idle()] * n_idle, vm, out_shape, name)


def exchange(x, axis="seq", groups=GROUPS):
    return lax.all_to_all(x, axis, 0, 0, tiled=True, axis_index_groups=groups)


def scan_groups(payload, reverse, first=(), second=()):
    recv = exchange(payload)
    total = small_call(
        functools.partial(k_total, reverse=reverse), 1, len(first), sds((NG * PR, D)), "total"
    )(recv, *first)
    totals = exchange(total, "seq", COLUMNS)
    rows = PR if reverse else CH
    back = small_call(
        functools.partial(k_carry, reverse=reverse), 2, len(second), sds((G * rows, D)), "carry"
    )(recv, totals, *second)
    return exchange(back)


def body(queries, key_vectors, value_vectors, out_grad, norm_gain, decay_rates, segment_ids):
    hb, sc = head_block(), scalars()
    big = 9 * 2 * L * L * D * NH
    flat = pltpu.VMEM((L, NH * D), F32)
    q, k, v, rates, segs = far(queries, key_vectors, value_vectors, decay_rates, segment_ids)
    vm, work = near_block(), idle()
    payload = one_call(
        k_state,
        [sc, sc, work, work],
        vm,
        sds((G * PR, D)),
        "state",
        big // 6,
        [pltpu.VMEM((L, NH * D), F32)] * 2 + [pltpu.SemaphoreType.DMA((2 * NH,))],
    )(segs, rates, k, v)
    local_out, bnd, con = heads_call(
        k_local,
        [sc, sc, hb, hb, hb, whole(NH * D)],
        [hb, sc, whole(16, D)],
        [flat, pltpu.HBM((8,), jnp.int32), pltpu.VMEM((16, D), F32)],
        big,
        name="local",
    )(segs, rates, q, k, v, *far(norm_gain))
    (bnd,) = far(bnd)
    (con,) = near(con)
    carry = scan_groups(payload, False)
    out, red = one_call(
        k_norm, [vm] * 5, [vm, vm], [flat, sds((64, D))], "norm", big // 6
    )(con, queries, carry, *near(local_out), out_grad)
    sums = exchange(red, "head", None)
    grad_out, payload = one_call(
        k_grad,
        [vm] * 5,
        [vm, vm],
        [flat, sds((G * PR, D))],
        "grad",
        big // 6,
    )(con, sums, out_grad, *near(out), queries)
    (grad_out,) = near(grad_out)
    dq, dk_local = heads_call(
        k_pgrad,
        [sc, sc, hb, hb, hb, hb, rows_block(D)],
        [hb, hb],
        [pltpu.HBM((L, NH * D), BF16), pltpu.HBM((L, NH * D), F32)],
        big,
        name="pgrad",
    )(bnd, rates, q, k, v, *far(grad_out), carry)
    dv_local = heads_call(
        k_vgrad, [sc, sc, hb, hb, hb], hb, flat, big // 2, name="vgrad"
    )(bnd, rates, q, k, grad_out)
    back = scan_groups(payload, True, (dv_local,))
    dk, dv, gain_grad = one_call(
        k_final,
        [vm, vm, vm, vm, work, vm],
        [work, work, vm],
        [pltpu.HBM((L, NH * D), BF16)] * 2 + [sds((NH * D,))],
        "final",
        big // 6,
        [pltpu.VMEM((L, NH * D), t) for t in (F32, BF16, BF16)]
        + [pltpu.SemaphoreType.DMA((3 * NH,))],
    )(con, key_vectors, value_vectors, back, *far(dk_local), *near(dv_local))
    return dq, dk, dv, gain_grad


def solution(mesh):
    return jax.shard_map(
        body,
        mesh=mesh,
        in_specs=(
            P("seq", "head"),
            P("seq", "head"),
            P("seq", "head"),
            P("seq", "head"),
            P("head"),
            P("head"),
            P("seq"),
        ),
        out_specs=(P("seq", "head"), P("seq", "head"), P("seq", "head"), P("head")),
        check_vma=False,
    )
```

time: 115 us -> 107 us (0.930)
  blocking collectives: 26.9 us -> 53.9 us
  starting transfers between devices: 31.6 us -> 18 us
  waiting for transfers between devices: 15.9 us -> 3.78 us
  Pallas kernels: 38.6 us -> 29.5 us
    all_to_all x2 -> x4, blocking collectives: 26.9 us -> 53.9 us  [exchange(): return lax.all_to_all(x, axis, 0, 0, tiled=True, axis_index_groups=groups)]
    all_to_all x5 -> x3, starting transfers between devices: 31.6 us -> 18 us  [exchange(): return lax.all_to_all(x, axis, 0, 0, tiled=True, axis_index_groups=groups)]
    all_to_all x5 -> x3, waiting for transfers between devices: 15.9 us -> 3.78 us  [exchange(): return lax.all_to_all(x, axis, 0, 0, tiled=True, axis_index_groups=groups)]
    pallas_call x12 -> x10, Pallas kernels: 33.4 us -> 24.3 us  [the longest x1 7.51 us: body(): heads_call(k_pgrad, [sc, sc, hb, hb, hb, hb, rows_block(D)], [hb, hb], [p...]
  transfers between devices with their start and end apart: 5 -> 3, of which waited for: 5 -> 3; matrix products, arithmetic and copies ran while one was open for 0% -> 0% of each run, Pallas kernels for 19% -> 18%
where the time goes in v1:
time: 107 us; the launch traced here: 106 us
  blocking collectives  53.9 us (50%)
  Pallas kernels  29.5 us (28%)
  starting transfers between devices  18 us (17%)
  waiting for transfers between devices  3.78 us (4%)
    all_to_all x4, blocking collectives, exchange(): return lax.all_to_all(x, axis, 0, 0, tiled=True, axis_index_groups=groups)  53.9 us
    all_to_all x3, starting transfers between devices, exchange(): return lax.all_to_all(x, axis, 0, 0, tiled=True, axis_index_groups=groups)  18 us
    pallas_call x1, Pallas kernels, body(): heads_call(k_pgrad, [sc, sc, hb, hb, hb, hb, rows_block(D)], [hb, hb], [p...  7.51 us
    pallas_call x1, Pallas kernels, body(): heads_call(k_local, [sc, sc, hb, hb, hb, whole(NH * D)], [hb, sc, whole(1...  6.19 us
    pallas_call x1, Pallas kernels, body(): heads_call(k_vgrad, [sc, sc, hb, hb, hb], hb, flat, big // 2, name='vgrad')  5.15 us
    all_to_all x3, waiting for transfers between devices, exchange(): return lax.all_to_all(x, axis, 0, 0, tiled=True, axis_index_groups=groups)  3.78 us
    pallas_call x1, Pallas kernels, body(): one_call(k_final, [vm, vm, vm, vm, work, vm], [work, work, vm], [pltpu.HB...  3.51 us
    pallas_call x1, Pallas kernels, body(): one_call(k_state, [sc, sc, work, work], vm, sds((G * PR, D)), 'state', bi...  3.08 us
  transfers between devices with their start and end apart: 3, of which 3 were waited for; matrix products, arithmetic and copies ran while one was open for 0% of the time, Pallas kernels for 18%

profile of v1, /device:TPU:1, one launch (start us, length us, event | category | flops | bytes accessed | tf_op | source)
XLA Modules:
  0.0 106.0 jit_solution(2263449251333522425)
XLA Ops:
  0.6 3.1 %state.1 = f32[640,128]{1,0:T(8,128)S(1)} custom-call(s32[384]{0:T(512)} %seg_ref.3, f32[4]{0:T(128)} %rate_ref.7, f32[384,512]{1,0:T(8,128)} %k_ref.7, f32[384,512]{1,0:T(8,128)} %v_ref.5), custom_call_target="tpu_custom_call" | custom-call | flops 226492416 | bytes 524288 | tf_op jit(solution)/shard_map/state/pallas_call | solution.py:428
  3.7 17.0 %all_to_all.77 = f32[16,40,128]{2,1,0:T(8,128)S(1)} all-to-all(f32[16,40,128]{2,1,0:T(8,128)S(1)} %bitcast.18), channel_id=1, replica_groups={{0,8,16,24,32,40,48,56,64,72,80,88,96,104,112,120},{128,136,144,152,160..., dimensions={0} | all-to-all | bytes 655360 | tf_op jit(solution)/shard_map/all_to_all | solution.py:406
  20.7 0.1 total.2
  20.8 14.1 %all_to_all.78 = f32[4,40,128]{2,1,0:T(8,128)S(1)} all-to-all(f32[4,40,128]{2,1,0:T(8,128)S(1)} %bitcast.23), channel_id=1, replica_groups={{0,128,256,384},{8,136,264,392},{16,144,272,400},{24,152,280,408},{32,1..., dimensions={0} | all-to-all | bytes 163840 | tf_op jit(solution)/shard_map/all_to_all | solution.py:406
  34.9 0.8 carry.2
  35.6 6.0 %all-to-all-start.2 = ((f32[16,32,128]{2,1,0:T(8,128)}), f32[16,32,128]{2,1,0:T(8,128)S(1)}, u32[]{:S(2)}, u32[]{:S(2)}) async-start(f32[16,32,128]{2,1,0:T(8,128)} %bitcast.4), calls=%async_computation.2 | async-start | bytes 524288 | tf_op jit(solution)/shard_map/all_to_all | solution.py:406
  41.6 0.0 copy-start.1
  41.6 0.0 copy-start.3
  41.7 6.2 %local.1 = (f32[384,512]{1,0:T(8,128)S(1)}, s32[8]{0:T(128)}, f32[16,128]{1,0:T(8,128)S(1)}) custom-call(s32[384]{0:T(512)} %seg_ref.3, f32[4]{0:T(128)} %rate_ref.7, f32[384,512]{1,0:T(8,128)} %q_ref.9, f32[384,512]{1,0:T(8,128)} %k_ref.7, f32[384,512]{1,0:T(8,128)} %v_ref.5, f32[512]{0:T(512)} %gain_ref.1), custom_call_target="tpu_custom_call" | custom-call | flops 1358954496 | bytes 3145728 | tf_op jit(solution)/shard_map/local/pallas_call | solution.py:437
  47.9 1.1 all-to-all-done.2
  48.9 0.0 copy-done.1
  48.9 0.0 copy-done.3
  48.9 0.8 norm.1
  49.7 13.5 %all_to_all.79 = f32[8,8,128]{2,1,0:T(8,128)S(1)} all-to-all(f32[8,8,128]{2,1,0:T(8,128)S(1)} %bitcast.27), channel_id=1, replica_groups=mesh['seq'=64,'head'=8] {'head'}, dimensions={0} | all-to-all | bytes 65536 | tf_op jit(solution)/shard_map/all_to_all | solution.py:406
  63.2 1.6 %grad.1 = (f32[384,512]{1,0:T(8,128)S(1)}, f32[640,128]{1,0:T(8,128)}) custom-call(f32[16,128]{1,0:T(8,128)S(1)} %get-tuple-element.17.con_ref, f32[64,128]{1,0:T(8,128)S(1)} %bitcast.26, f32[384,512]{1,0:T(8,128)S(1)} %copy-done.3, f32[384,512]{1,0:T(8,128)S(1)} %get-tuple-element.20.o_ref, f32[384,512]{1,0:T(8,128)S(1)} %copy-done.1), custom_call_target="tpu_custom_call" | custom-call | flops 226492416 | bytes 524288 | tf_op jit(solution)/shard_map/grad/pallas_call | solution.py:452
  64.8 0.0 copy-start.4
  64.8 6.2 %all-to-all-start.4 = ((f32[16,40,128]{2,1,0:T(8,128)}), f32[16,40,128]{2,1,0:T(8,128)S(1)}, u32[]{:S(2)}, u32[]{:S(2)}) async-start(f32[16,40,128]{2,1,0:T(8,128)} %bitcast.8), calls=%async_computation.4 | async-start | bytes 655360 | tf_op jit(solution)/shard_map/all_to_all | solution.py:406
  71.0 5.2 %vgrad.1.rest_0_.dvl_ref = f32[384,512]{1,0:T(8,128)S(1)} custom-call(s32[8]{0:T(128)} %get-tuple-element.16.bnd_ref, f32[4]{0:T(128)} %rate_ref.7, f32[384,512]{1,0:T(8,128)} %q_ref.9, f32[384,512]{1,0:T(8,128)} %k_ref.7, f32[384,512]{1,0:T(8,128)S(1)} %get-tuple-element.21.do_ref), custom_call_target="tpu_custom_call" | custom-call | flops 679477248 | bytes 3145728 | tf_op jit(solution)/shard_map/vgrad/pallas_call | solution.py:469
  76.1 0.0 copy-done.4
  76.1 2.5 %all-to-all-done.4 = f32[16,40,128]{2,1,0:T(8,128)S(1)} async-done(((f32[16,40,128]{2,1,0:T(8,128)}), f32[16,40,128]{2,1,0:T(8,128)S(1)}, u32[]{:S(2)}, u32[]{:S(2)}) %all-to-all-start.4) | async-done | bytes 327712 | tf_op jit(solution)/shard_map/all_to_all | solution.py:406
  78.6 0.1 total.3
  78.7 9.3 %all_to_all.80 = f32[4,40,128]{2,1,0:T(8,128)S(1)} all-to-all(f32[4,40,128]{2,1,0:T(8,128)S(1)} %bitcast.22), channel_id=1, replica_groups={{0,128,256,384},{8,136,264,392},{16,144,272,400},{24,152,280,408},{32,1..., dimensions={0} | all-to-all | bytes 163840 | tf_op jit(solution)/shard_map/all_to_all | solution.py:406
  88.0 0.8 carry.3
  88.8 5.8 %all-to-all-start.6 = ((f32[16,40,128]{2,1,0:T(8,128)}), f32[16,40,128]{2,1,0:T(8,128)S(1)}, u32[]{:S(2)}, u32[]{:S(2)}) async-start(f32[16,40,128]{2,1,0:T(8,128)} %bitcast.12), calls=%async_computation.6 | async-start | bytes 655360 | tf_op jit(solution)/shard_map/all_to_all | solution.py:406
  94.7 0.0 copy-start
  94.7 0.0 copy-start.2
  94.7 7.5 %pgrad.1 = (bf16[384,512]{1,0:T(8,128)(2,1)}, f32[384,512]{1,0:T(8,128)}) custom-call(s32[8]{0:T(128)} %get-tuple-element.16.bnd_ref, f32[4]{0:T(128)} %rate_ref.7, f32[384,512]{1,0:T(8,128)} %q_ref.9, f32[384,512]{1,0:T(8,128)} %k_ref.7, f32[384,512]{1,0:T(8,128)} %v_ref.5, f32[384,512]{1,0:T(8,128)} %copy-done.4, f32[512,128]{1,0:T(8,128)S(1)} %bitcast.21), custom_call_target="tpu_custom_call" | custom-call | flops 1358954496 | bytes 3145728 | tf_op jit(solution)/shard_map/pgrad/pallas_call | solution.py:461
  102.2 0.2 all-to-all-done.6
  102.4 0.0 copy-done
  102.4 0.0 copy-done.2
  102.4 3.5 %final.1 = (bf16[384,512]{1,0:T(8,128)(2,1)}, bf16[384,512]{1,0:T(8,128)(2,1)}, f32[512]{0:T(512)}) custom-call(f32[16,128]{1,0:T(8,128)S(1)} %get-tuple-element.17.con_ref, f32[384,512]{1,0:T(8,128)S(1)} %copy-done, f32[384,512]{1,0:T(8,128)S(1)} %copy-done.2, f32[640,128]{1,0:T(8,128)S(1)} %bitcast.19, f32[384,512]{1,0:T(8,128)} %get-tuple-element.24.dkl_hbm, ...), custom_call_target="tpu_custom_call" | custom-call | flops 226492416 | bytes 524288 | tf_op jit(solution)/shard_map/final/pallas_call | solution.py:473
Async XLA Ops:
  35.6 13.3 %all-to-all-start.2 = ((f32[16,32,128]{2,1,0:T(8,128)}), f32[16,32,128]{2,1,0:T(8,128)S(1)}, u32[]{:S(2)}, u32[]{:S(2)}) async-start(f32[16,32,128]{2,1,0:T(8,128)} %bitcast.4), calls=%async_computation.2 | async-start | bytes 524288 | tf_op jit(solution)/shard_map/all_to_all | solution.py:406
  41.6 7.3 %copy-start.1 = (f32[384,512]{1,0:T(8,128)S(1)}, f32[384,512]{1,0:T(8,128)}, u32[]{:S(2)}) copy-start(f32[384,512]{1,0:T(8,128)} %q_ref.9) | copy-start | bytes 2359300
  41.6 7.3 %copy-start.3 = (f32[384,512]{1,0:T(8,128)S(1)}, f32[384,512]{1,0:T(8,128)}, u32[]{:S(2)}) copy-start(f32[384,512]{1,0:T(8,128)} %og_ref.3) | copy-start | bytes 2359300
  64.8 11.4 %copy-start.4 = (f32[384,512]{1,0:T(8,128)}, f32[384,512]{1,0:T(8,128)S(1)}, u32[]{:S(2)}) copy-start(f32[384,512]{1,0:T(8,128)S(1)} %get-tuple-element.21.do_ref) | copy-start | bytes 2359300
  64.8 13.9 %all-to-all-start.4 = ((f32[16,40,128]{2,1,0:T(8,128)}), f32[16,40,128]{2,1,0:T(8,128)S(1)}, u32[]{:S(2)}, u32[]{:S(2)}) async-start(f32[16,40,128]{2,1,0:T(8,128)} %bitcast.8), calls=%async_computation.4 | async-start | bytes 655360 | tf_op jit(solution)/shard_map/all_to_all | solution.py:406
  88.8 13.6 %all-to-all-start.6 = ((f32[16,40,128]{2,1,0:T(8,128)}), f32[16,40,128]{2,1,0:T(8,128)S(1)}, u32[]{:S(2)}, u32[]{:S(2)}) async-start(f32[16,40,128]{2,1,0:T(8,128)} %bitcast.12), calls=%async_computation.6 | async-start | bytes 655360 | tf_op jit(solution)/shard_map/all_to_all | solution.py:406
  94.7 7.7 %copy-start = (f32[384,512]{1,0:T(8,128)S(1)}, f32[384,512]{1,0:T(8,128)}, u32[]{:S(2)}) copy-start(f32[384,512]{1,0:T(8,128)} %k_ref.7) | copy-start | bytes 2359300
  94.7 7.7 %copy-start.2 = (f32[384,512]{1,0:T(8,128)S(1)}, f32[384,512]{1,0:T(8,128)}, u32[]{:S(2)}) copy-start(f32[384,512]{1,0:T(8,128)} %v_ref.5) | copy-start | bytes 2359300

commit v2 on v1

--- a/solution.py
+++ b/solution.py
@@ -73,7 +73,13 @@
     return slice(h * D, (h + 1) * D)
 
 
-def k_state(seg_ref, rate_ref, k_hbm, v_hbm, out_ref, k_ref, v_ref, sems):
+def k_state(seg_hbm, rate_hbm, k_hbm, v_hbm, out_ref, k_ref, v_ref, seg_ref, rate_ref, sems):
+    small = [
+        pltpu.make_async_copy(seg_hbm, seg_ref, sems.at[2 * NH]),
+        pltpu.make_async_copy(rate_hbm, rate_ref, sems.at[2 * NH + 1]),
+    ]
+    for copy in small:
+        copy.start()
     copies = []
     for h in range(NH):
         for t, (src, dst) in enumerate(((k_hbm, k_ref), (v_hbm, v_ref))):
@@ -81,6 +87,8 @@
                 pltpu.make_async_copy(src.at[:, head(h)], dst.at[:, head(h)], sems.at[2 * h + t])
             )
             copies[-1].start()
+    for copy in small:
+        copy.wait()
     first, last = seg_ref[0], seg_ref[L - 1]
     start = first_at_least(seg_ref, last)
     i = rows_iota()
@@ -296,15 +304,9 @@
 
 
 def k_final(
-    con_ref, k_ref, v_ref, st_ref, dkl_hbm, dvl_ref, dk_hbm, dv_hbm, gg_ref,
-    dkl_ref, dk_ref, dv_ref, sems,
+    con_ref, k_ref, v_ref, st_ref, dkl_ref, dvl_ref, dk_hbm, dv_hbm, gg_ref, dk_ref, dv_ref, sems
 ):
-    loads, stores = [], []
-    for h in range(NH):
-        loads.append(
-            pltpu.make_async_copy(dkl_hbm.at[:, head(h)], dkl_ref.at[:, head(h)], sems.at[h])
-        )
-        loads[-1].start()
+    stores = []
     i = rows_iota().astype(F32)
     inside = i >= con_ref[5:6, :]
     back = float(L) - i
@@ -313,18 +315,13 @@
         bases = [(h * PER + t) * PR for t in range(PER)]
         ss = split(jnp.concatenate([st_ref[b : b + CH, :] for b in bases], axis=0))
         gg_ref[head(h)] = st_ref[bases[0] + CH + 3, :]
-        for t in range(2):
-            if t == 0:
-                x = dvl_ref[:, head(h)] + c * dot3(split(k_ref[:, head(h)]), ss, 1, 0)
-                buf, far_ref = dv_ref, dv_hbm
-            else:
-                loads[h].wait()
-                x = dkl_ref[:, head(h)] + c * dot3(split(v_ref[:, head(h)]), ss, 1, 1)
-                buf, far_ref = dk_ref, dk_hbm
+        dk = dkl_ref[:, head(h)] + c * dot3(split(v_ref[:, head(h)]), ss, 1, 1)
+        dv = dvl_ref[:, head(h)] + c * dot3(split(k_ref[:, head(h)]), ss, 1, 0)
+        for t, (x, buf, out) in enumerate(((dk, dk_ref, dk_hbm), (dv, dv_ref, dv_hbm))):
             buf[:, head(h)] = x.astype(BF16)
             stores.append(
                 pltpu.make_async_copy(
-                    buf.at[:, head(h)], far_ref.at[:, head(h)], sems.at[NH + 2 * h + t]
+                    buf.at[:, head(h)], out.at[:, head(h)], sems.at[2 * h + t]
                 )
             )
             stores[-1].start()
@@ -427,12 +424,13 @@
     vm, work = near_block(), idle()
     payload = one_call(
         k_state,
-        [sc, sc, work, work],
+        [work] * 4,
         vm,
         sds((G * PR, D)),
         "state",
         big // 6,
-        [pltpu.VMEM((L, NH * D), F32)] * 2 + [pltpu.SemaphoreType.DMA((2 * NH,))],
+        [pltpu.VMEM((L, NH * D), F32)] * 2
+        + [SMEM((L,), jnp.int32), SMEM((NH,), F32), pltpu.SemaphoreType.DMA((2 * NH + 2,))],
     )(segs, rates, k, v)
     local_out, bnd, con = heads_call(
         k_local,
@@ -462,24 +460,23 @@
         k_pgrad,
         [sc, sc, hb, hb, hb, hb, rows_block(D)],
         [hb, hb],
-        [pltpu.HBM((L, NH * D), BF16), pltpu.HBM((L, NH * D), F32)],
+        [pltpu.HBM((L, NH * D), BF16), flat],
         big,
         name="pgrad",
-    )(bnd, rates, q, k, v, *far(grad_out), carry)
+    )(bnd, rates, q, k, v, grad_out, carry)
     dv_local = heads_call(
         k_vgrad, [sc, sc, hb, hb, hb], hb, flat, big // 2, name="vgrad"
-    )(bnd, rates, q, k, grad_out)
-    back = scan_groups(payload, True, (dv_local,))
+    )(bnd, rates, q, k, *far(grad_out))
+    back = scan_groups(payload, True, (dk_local,))
     dk, dv, gain_grad = one_call(
         k_final,
-        [vm, vm, vm, vm, work, vm],
+        [vm] * 6,
         [work, work, vm],
         [pltpu.HBM((L, NH * D), BF16)] * 2 + [sds((NH * D,))],
         "final",
         big // 6,
-        [pltpu.VMEM((L, NH * D), t) for t in (F32, BF16, BF16)]
-        + [pltpu.SemaphoreType.DMA((3 * NH,))],
-    )(con, key_vectors, value_vectors, back, *far(dk_local), *near(dv_local))
+        [pltpu.VMEM((L, NH * D), BF16)] * 2 + [pltpu.SemaphoreType.DMA((2 * NH,))],
+    )(con, key_vectors, value_vectors, back, *near(dk_local, dv_local))
     return dq, dk, dv, gain_grad
 
 

time: 107 us -> 106 us (level)
  Pallas kernels: 29.5 us -> 27.5 us
  starting transfers between devices: 18 us -> 19.1 us
    pallas_call x2, Pallas kernels: 6.59 us -> 4.54 us  [the longest x1 2.41 us: body(): one_call(k_state, [work] * 4, vm, sds((G * PR, D)), 'state', big // 6, [p...]
where the time goes in v2:
time: 106 us; the launch traced here: 105 us
  blocking collectives  53.9 us (51%)
  Pallas kernels  27.5 us (26%)
  starting transfers between devices  19.1 us (18%)
  waiting for transfers between devices  3.67 us (3%)
    all_to_all x4, blocking collectives, exchange(): return lax.all_to_all(x, axis, 0, 0, tiled=True, axis_index_groups=groups)  53.9 us
    all_to_all x3, starting transfers between devices, exchange(): return lax.all_to_all(x, axis, 0, 0, tiled=True, axis_index_groups=groups)  19.1 us
    pallas_call x1, Pallas kernels, body(): heads_call(k_pgrad, [sc, sc, hb, hb, hb, hb, rows_block(D)], [hb, hb], [p...  7.27 us
    pallas_call x1, Pallas kernels, body(): heads_call(k_local, [sc, sc, hb, hb, hb, whole(NH * D)], [hb, sc, whole(1...  6.18 us
    pallas_call x1, Pallas kernels, body(): heads_call(k_vgrad, [sc, sc, hb, hb, hb], hb, flat, big // 2, name='vgrad')  5.44 us
    all_to_all x3, waiting for transfers between devices, exchange(): return lax.all_to_all(x, axis, 0, 0, tiled=True, axis_index_groups=groups)  3.67 us
    pallas_call x1, Pallas kernels, body(): one_call(k_state, [work] * 4, vm, sds((G * PR, D)), 'state', big // 6, [p...  2.41 us
    pallas_call x1, Pallas kernels, body(): one_call(k_final, [vm] * 6, [work, work, vm], [pltpu.HBM((L, NH * D), BF1...  2.14 us
  transfers between devices with their start and end apart: 3, of which 3 were waited for; matrix products, arithmetic and copies ran while one was open for 0% of the time, Pallas kernels for 18%

profile of v2, /device:TPU:1, one launch (start us, length us, event | category | flops | bytes accessed | tf_op | source)
XLA Modules:
  0.0 104.9 jit_solution(7914924009823846748)
XLA Ops:
  0.6 2.4 %state.1 = f32[640,128]{1,0:T(8,128)S(1)} custom-call(s32[384]{0:T(512)} %seg_hbm.1, f32[4]{0:T(128)} %rate_ref.5, f32[384,512]{1,0:T(8,128)} %k_ref.7, f32[384,512]{1,0:T(8,128)} %v_ref.5), custom_call_target="tpu_custom_call" | custom-call | flops 226492416 | bytes 524288 | tf_op jit(solution)/shard_map/state/pallas_call | solution.py:425
  3.0 17.0 %all_to_all.77 = f32[16,40,128]{2,1,0:T(8,128)S(1)} all-to-all(f32[16,40,128]{2,1,0:T(8,128)S(1)} %bitcast.18), channel_id=1, replica_groups={{0,8,16,24,32,40,48,56,64,72,80,88,96,104,112,120},{128,136,144,152,160..., dimensions={0} | all-to-all | bytes 655360 | tf_op jit(solution)/shard_map/all_to_all | solution.py:403
  20.1 0.1 total.2
  20.1 14.1 %all_to_all.78 = f32[4,40,128]{2,1,0:T(8,128)S(1)} all-to-all(f32[4,40,128]{2,1,0:T(8,128)S(1)} %bitcast.23), channel_id=1, replica_groups={{0,128,256,384},{8,136,264,392},{16,144,272,400},{24,152,280,408},{32,1..., dimensions={0} | all-to-all | bytes 163840 | tf_op jit(solution)/shard_map/all_to_all | solution.py:403
  34.2 0.8 carry.2
  35.0 6.0 %all-to-all-start.2 = ((f32[16,32,128]{2,1,0:T(8,128)}), f32[16,32,128]{2,1,0:T(8,128)S(1)}, u32[]{:S(2)}, u32[]{:S(2)}) async-start(f32[16,32,128]{2,1,0:T(8,128)} %bitcast.4), calls=%async_computation.2 | async-start | bytes 524288 | tf_op jit(solution)/shard_map/all_to_all | solution.py:403
  41.0 0.0 copy-start.1
  41.0 0.0 copy-start.3
  41.0 6.2 %local.1 = (f32[384,512]{1,0:T(8,128)S(1)}, s32[8]{0:T(128)}, f32[16,128]{1,0:T(8,128)S(1)}) custom-call(s32[384]{0:T(512)} %seg_hbm.1, f32[4]{0:T(128)} %rate_ref.5, f32[384,512]{1,0:T(8,128)} %q_ref.9, f32[384,512]{1,0:T(8,128)} %k_ref.7, f32[384,512]{1,0:T(8,128)} %v_ref.5, f32[512]{0:T(512)} %gain_ref.1), custom_call_target="tpu_custom_call" | custom-call | flops 1358954496 | bytes 3145728 | tf_op jit(solution)/shard_map/local/pallas_call | solution.py:435
  47.2 1.1 %all-to-all-done.2 = f32[16,32,128]{2,1,0:T(8,128)S(1)} async-done(((f32[16,32,128]{2,1,0:T(8,128)}), f32[16,32,128]{2,1,0:T(8,128)S(1)}, u32[]{:S(2)}, u32[]{:S(2)}) %all-to-all-start.2) | async-done | bytes 262176 | tf_op jit(solution)/shard_map/all_to_all | solution.py:403
  48.2 0.0 copy-done.1
  48.2 0.0 copy-done.3
  48.2 0.8 norm.1
  49.0 13.5 %all_to_all.79 = f32[8,8,128]{2,1,0:T(8,128)S(1)} all-to-all(f32[8,8,128]{2,1,0:T(8,128)S(1)} %bitcast.27), channel_id=1, replica_groups=mesh['seq'=64,'head'=8] {'head'}, dimensions={0} | all-to-all | bytes 65536 | tf_op jit(solution)/shard_map/all_to_all | solution.py:403
  62.5 1.6 %grad.1 = (f32[384,512]{1,0:T(8,128)S(1)}, f32[640,128]{1,0:T(8,128)}) custom-call(f32[16,128]{1,0:T(8,128)S(1)} %get-tuple-element.17.con_ref, f32[64,128]{1,0:T(8,128)S(1)} %bitcast.26, f32[384,512]{1,0:T(8,128)S(1)} %copy-done.3, f32[384,512]{1,0:T(8,128)S(1)} %get-tuple-element.20.o_ref, f32[384,512]{1,0:T(8,128)S(1)} %copy-done.1), custom_call_target="tpu_custom_call" | custom-call | flops 226492416 | bytes 524288 | tf_op jit(solution)/shard_map/grad/pallas_call | solution.py:450
  64.1 0.0 copy-start.4
  64.1 6.2 %all-to-all-start.4 = ((f32[16,40,128]{2,1,0:T(8,128)}), f32[16,40,128]{2,1,0:T(8,128)S(1)}, u32[]{:S(2)}, u32[]{:S(2)}) async-start(f32[16,40,128]{2,1,0:T(8,128)} %bitcast.8), calls=%async_computation.4 | async-start | bytes 655360 | tf_op jit(solution)/shard_map/all_to_all | solution.py:403
  70.3 7.3 %pgrad.1 = (bf16[384,512]{1,0:T(8,128)(2,1)}, f32[384,512]{1,0:T(8,128)S(1)}) custom-call(s32[8]{0:T(128)} %get-tuple-element.16.bnd_ref, f32[4]{0:T(128)} %rate_ref.5, f32[384,512]{1,0:T(8,128)} %q_ref.9, f32[384,512]{1,0:T(8,128)} %k_ref.7, f32[384,512]{1,0:T(8,128)} %v_ref.5, f32[384,512]{1,0:T(8,128)S(1)} %get-tuple-element.21.do_ref, ...), custom_call_target="tpu_custom_call" | custom-call | flops 1358954496 | bytes 3145728 | tf_op jit(solution)/shard_map/pgrad/pallas_call | solution.py:459
  77.6 0.0 copy-done.4
  77.6 0.4 all-to-all-done.4
  78.0 0.1 total.3
  78.0 9.3 %all_to_all.80 = f32[4,40,128]{2,1,0:T(8,128)S(1)} all-to-all(f32[4,40,128]{2,1,0:T(8,128)S(1)} %bitcast.22), channel_id=1, replica_groups={{0,128,256,384},{8,136,264,392},{16,144,272,400},{24,152,280,408},{32,1..., dimensions={0} | all-to-all | bytes 163840 | tf_op jit(solution)/shard_map/all_to_all | solution.py:403
  87.4 0.8 carry.3
  88.2 6.9 %all-to-all-start.6 = ((f32[16,40,128]{2,1,0:T(8,128)}), f32[16,40,128]{2,1,0:T(8,128)S(1)}, u32[]{:S(2)}, u32[]{:S(2)}) async-start(f32[16,40,128]{2,1,0:T(8,128)} %bitcast.12), calls=%async_computation.6 | async-start | bytes 655360 | tf_op jit(solution)/shard_map/all_to_all | solution.py:403
  95.0 0.0 copy-start
  95.1 0.0 copy-start.2
  95.1 5.4 %vgrad.1.dvl_ref = f32[384,512]{1,0:T(8,128)S(1)} custom-call(s32[8]{0:T(128)} %get-tuple-element.16.bnd_ref, f32[4]{0:T(128)} %rate_ref.5, f32[384,512]{1,0:T(8,128)} %q_ref.9, f32[384,512]{1,0:T(8,128)} %k_ref.7, f32[384,512]{1,0:T(8,128)} %copy-done.4), custom_call_target="tpu_custom_call" | custom-call | flops 679477248 | bytes 3145728 | tf_op jit(solution)/shard_map/vgrad/pallas_call | solution.py:467
  100.5 2.2 %all-to-all-done.6 = f32[16,40,128]{2,1,0:T(8,128)S(1)} async-done(((f32[16,40,128]{2,1,0:T(8,128)}), f32[16,40,128]{2,1,0:T(8,128)S(1)}, u32[]{:S(2)}, u32[]{:S(2)}) %all-to-all-start.6) | async-done | bytes 327712 | tf_op jit(solution)/shard_map/all_to_all | solution.py:403
  102.7 0.0 copy-done
  102.7 0.0 copy-done.2
  102.7 2.1 %final.1 = (bf16[384,512]{1,0:T(8,128)(2,1)}, bf16[384,512]{1,0:T(8,128)(2,1)}, f32[512]{0:T(512)}) custom-call(f32[16,128]{1,0:T(8,128)S(1)} %get-tuple-element.17.con_ref, f32[384,512]{1,0:T(8,128)S(1)} %copy-done, f32[384,512]{1,0:T(8,128)S(1)} %copy-done.2, f32[640,128]{1,0:T(8,128)S(1)} %bitcast.19, f32[384,512]{1,0:T(8,128)S(1)} %get-tuple-element.24.rest_0_.dkl_ref, ...), custom_call_target="tpu_custom_call" | custom-call | flops 226492416 | bytes 524288 | tf_op jit(solution)/shard_map/final/pallas_call | solution.py:471
Async XLA Ops:
  35.0 13.3 %all-to-all-start.2 = ((f32[16,32,128]{2,1,0:T(8,128)}), f32[16,32,128]{2,1,0:T(8,128)S(1)}, u32[]{:S(2)}, u32[]{:S(2)}) async-start(f32[16,32,128]{2,1,0:T(8,128)} %bitcast.4), calls=%async_computation.2 | async-start | bytes 524288 | tf_op jit(solution)/shard_map/all_to_all | solution.py:403
  41.0 7.3 %copy-start.1 = (f32[384,512]{1,0:T(8,128)S(1)}, f32[384,512]{1,0:T(8,128)}, u32[]{:S(2)}) copy-start(f32[384,512]{1,0:T(8,128)} %q_ref.9) | copy-start | bytes 2359300
  41.0 7.3 %copy-start.3 = (f32[384,512]{1,0:T(8,128)S(1)}, f32[384,512]{1,0:T(8,128)}, u32[]{:S(2)}) copy-start(f32[384,512]{1,0:T(8,128)} %og_ref.3) | copy-start | bytes 2359300
  64.1 13.5 %copy-start.4 = (f32[384,512]{1,0:T(8,128)}, f32[384,512]{1,0:T(8,128)S(1)}, u32[]{:S(2)}) copy-start(f32[384,512]{1,0:T(8,128)S(1)} %get-tuple-element.21.do_ref) | copy-start | bytes 2359300
  64.1 13.9 %all-to-all-start.4 = ((f32[16,40,128]{2,1,0:T(8,128)}), f32[16,40,128]{2,1,0:T(8,128)S(1)}, u32[]{:S(2)}, u32[]{:S(2)}) async-start(f32[16,40,128]{2,1,0:T(8,128)} %bitcast.8), calls=%async_computation.4 | async-start | bytes 655360 | tf_op jit(solution)/shard_map/all_to_all | solution.py:403
  88.2 14.5 %all-to-all-start.6 = ((f32[16,40,128]{2,1,0:T(8,128)}), f32[16,40,128]{2,1,0:T(8,128)S(1)}, u32[]{:S(2)}, u32[]{:S(2)}) async-start(f32[16,40,128]{2,1,0:T(8,128)} %bitcast.12), calls=%async_computation.6 | async-start | bytes 655360 | tf_op jit(solution)/shard_map/all_to_all | solution.py:403
  95.0 7.7 %copy-start = (f32[384,512]{1,0:T(8,128)S(1)}, f32[384,512]{1,0:T(8,128)}, u32[]{:S(2)}) copy-start(f32[384,512]{1,0:T(8,128)} %k_ref.7) | copy-start | bytes 2359300
  95.1 7.7 %copy-start.2 = (f32[384,512]{1,0:T(8,128)S(1)}, f32[384,512]{1,0:T(8,128)}, u32[]{:S(2)}) copy-start(f32[384,512]{1,0:T(8,128)} %v_ref.5) | copy-start | bytes 2359300

commit v3 on v2

--- a/solution.py
+++ b/solution.py
@@ -56,16 +56,26 @@
     return s
 
 
-def notes(first, last, rate, gain=0.0):
+GAIN = 3
+
+
+def notes(first, last, rate, gains=()):
     row = lax.broadcasted_iota(jnp.int32, (8, D), 0)
-    rest = jnp.where(row == 2, rate, jnp.where(row == 3, gain, 0.0))
-    return jnp.where(row == 0, first, jnp.where(row == 1, last, rest))
-
-
-def put_state(out_ref, h, state, note):
+    tile = jnp.where(row == 0, first, jnp.where(row == 1, last, jnp.where(row == 2, rate, 0.0)))
+    for t, gain in enumerate(gains):
+        tile = jnp.where(row == GAIN + t, gain, tile)
+    return tile
+
+
+def put_state(out_ref, h, state):
     for t in range(PER):
         base = (h * PER + t) * PR
         out_ref[base : base + CH, :] = state[t * CH : (t + 1) * CH]
+
+
+def put_note(out_ref, h, note):
+    for t in range(PER):
+        base = (h * PER + t) * PR
         out_ref[base + CH : base + PR, :] = note
 
 
@@ -99,8 +109,8 @@
         copies[2 * h].wait()
         copies[2 * h + 1].wait()
         u = dot3(split(k_ref[:, head(h)] * b), split(v_ref[:, head(h)]), 0, 0)
-        note = notes(first.astype(F32), last.astype(F32), rate)
-        put_state(out_ref, h, u, note)
+        put_state(out_ref, h, u)
+        put_note(out_ref, h, notes(first.astype(F32), last.astype(F32), rate))
 
 
 def weights(rate, bounds, rb):
@@ -176,14 +186,13 @@
     if reverse:
         for i in range(1, G):
             note = note + recv_ref[i * PR + CH : (i + 1) * PR, :]
-        out = jnp.where(row == 3, note, out)
+        out = jnp.where(row >= GAIN, note, out)
     t_ref[CH:PR, :] = out
     for t in range(1, NG):
         t_ref[t * PR : (t + 1) * PR, :] = t_ref[0:PR, :]
 
 
-def k_carry(recv_ref, t_ref, *rest, reverse):
-    out_ref = rest[-1]
+def k_carry(recv_ref, t_ref, out_ref, *rest, reverse):
     mine = lax.div(lax.axis_index("seq"), G)
     rate = recv_ref[CH + 2 : CH + 3, :]
     edge = G - 1 if reverse else 0
@@ -199,12 +208,11 @@
         power = jnp.maximum(gap, 0).astype(F32) * float(L * G)
         state = state + jnp.where(same, jnp.exp(-rate * power), 0.0) * t_ref[base : base + CH, :]
         gain = gain + t_ref[base + CH : base + PR, :]
-    rows = PR if reverse else CH
+    if reverse:
+        rest[0][...] = gain
 
     def take(i, s):
-        out_ref[i * rows : i * rows + CH, :] = s
-        if reverse:
-            out_ref[i * rows + CH : i * rows + PR, :] = gain
+        out_ref[i * CH : (i + 1) * CH, :] = s
 
     chain(recv_ref, state, reverse, take)
 
@@ -250,6 +258,7 @@
     i = rows_iota().astype(F32)
     inside = i < con_ref[4:5, :]
     first, last = con_ref[6:7, :], con_ref[7:8, :]
+    gains = []
     for h in range(NH):
         rate = con_ref[h : h + 1, :]
         rog = r * og_ref[:, head(h)]
@@ -258,8 +267,10 @@
         do_ref[:, head(h)] = do
         e = jnp.where(inside, jnp.exp(-rate * i), 0.0)
         v = dot3(split(q_ref[:, head(h)] * e), split(do), 0, 0)
-        part = jnp.sum(rog * o, axis=0, keepdims=True)
-        put_state(out_ref, h, v, notes(first, last, rate, part))
+        gains.append(jnp.sum(rog * o, axis=0, keepdims=True))
+        put_state(out_ref, h, v)
+    for h in range(NH):
+        put_note(out_ref, h, notes(first, last, con_ref[h : h + 1, :], gains))
 
 
 def k_pgrad(bnd_ref, rate_ref, q_ref, k_ref, v_ref, do_ref, c_ref, dq_ref, dk_ref):
@@ -304,7 +315,8 @@
 
 
 def k_final(
-    con_ref, k_ref, v_ref, st_ref, dkl_ref, dvl_ref, dk_hbm, dv_hbm, gg_ref, dk_ref, dv_ref, sems
+    con_ref, k_ref, v_ref, st_ref, dkl_ref, dvl_ref, gain_ref,
+    dk_hbm, dv_hbm, gg_ref, dk_ref, dv_ref, sems,
 ):
     stores = []
     i = rows_iota().astype(F32)
@@ -312,9 +324,8 @@
     back = float(L) - i
     for h in range(NH):
         c = jnp.where(inside, jnp.exp(-con_ref[h : h + 1, :] * back), 0.0)
-        bases = [(h * PER + t) * PR for t in range(PER)]
-        ss = split(jnp.concatenate([st_ref[b : b + CH, :] for b in bases], axis=0))
-        gg_ref[head(h)] = st_ref[bases[0] + CH + 3, :]
+        ss = split(st_ref[head(h), :])
+        gg_ref[head(h)] = gain_ref[GAIN + h, :]
         dk = dkl_ref[:, head(h)] + c * dot3(split(v_ref[:, head(h)]), ss, 1, 1)
         dv = dvl_ref[:, head(h)] + c * dot3(split(k_ref[:, head(h)]), ss, 1, 0)
         for t, (x, buf, out) in enumerate(((dk, dk_ref, dk_hbm), (dv, dv_ref, dv_hbm))):
@@ -403,17 +414,18 @@
     return lax.all_to_all(x, axis, 0, 0, tiled=True, axis_index_groups=groups)
 
 
-def scan_groups(payload, reverse, first=(), second=()):
+def scan_groups(payload, reverse, order=()):
+    vm = near_block()
     recv = exchange(payload)
     total = small_call(
-        functools.partial(k_total, reverse=reverse), 1, len(first), sds((NG * PR, D)), "total"
-    )(recv, *first)
+        functools.partial(k_total, reverse=reverse), 1, len(order), sds((NG * PR, D)), "total"
+    )(recv, *order)
     totals = exchange(total, "seq", COLUMNS)
-    rows = PR if reverse else CH
-    back = small_call(
-        functools.partial(k_carry, reverse=reverse), 2, len(second), sds((G * rows, D)), "carry"
-    )(recv, totals, *second)
-    return exchange(back)
+    shapes = [sds((G * CH, D))] + ([pltpu.VMEM((8, D), F32)] if reverse else [])
+    back, *gain = one_call(
+        functools.partial(k_carry, reverse=reverse), [vm] * 2, [vm] * len(shapes), shapes, "carry"
+    )(recv, totals)
+    return exchange(back), *near(*gain)
 
 
 def body(queries, key_vectors, value_vectors, out_grad, norm_gain, decay_rates, segment_ids):
@@ -442,7 +454,7 @@
     )(segs, rates, q, k, v, *far(norm_gain))
     (bnd,) = far(bnd)
     (con,) = near(con)
-    carry = scan_groups(payload, False)
+    (carry,) = scan_groups(payload, False)
     out, red = one_call(
         k_norm, [vm] * 5, [vm, vm], [flat, sds((64, D))], "norm", big // 6
     )(con, queries, carry, *near(local_out), out_grad)
@@ -467,16 +479,16 @@
     dv_local = heads_call(
         k_vgrad, [sc, sc, hb, hb, hb], hb, flat, big // 2, name="vgrad"
     )(bnd, rates, q, k, *far(grad_out))
-    back = scan_groups(payload, True, (dk_local,))
+    back, gain = scan_groups(payload, True, (dk_local,))
     dk, dv, gain_grad = one_call(
         k_final,
-        [vm] * 6,
+        [vm] * 7,
         [work, work, vm],
         [pltpu.HBM((L, NH * D), BF16)] * 2 + [sds((NH * D,))],
         "final",
         big // 6,
         [pltpu.VMEM((L, NH * D), BF16)] * 2 + [pltpu.SemaphoreType.DMA((2 * NH,))],
-    )(con, key_vectors, value_vectors, back, *near(dk_local, dv_local))
+    )(con, key_vectors, value_vectors, back, *near(dk_local, dv_local), gain)
     return dq, dk, dv, gain_grad
 
 

time: 106 us -> 105 us (level)
  no operation moved by 1% of the time
where the time goes in v3:
time: 105 us; the launch traced here: 104 us
  blocking collectives  53.9 us (51%)
  Pallas kernels  27.5 us (26%)
  starting transfers between devices  19.1 us (18%)
  waiting for transfers between devices  3.19 us (3%)
    all_to_all x4, blocking collectives, exchange(): return lax.all_to_all(x, axis, 0, 0, tiled=True, axis_index_groups=groups)  53.9 us
    all_to_all x3, starting transfers between devices, exchange(): return lax.all_to_all(x, axis, 0, 0, tiled=True, axis_index_groups=groups)  19.1 us
    pallas_call x1, Pallas kernels, body(): heads_call(k_pgrad, [sc, sc, hb, hb, hb, hb, rows_block(D)], [hb, hb], [p...  7.28 us
    pallas_call x1, Pallas kernels, body(): heads_call(k_local, [sc, sc, hb, hb, hb, whole(NH * D)], [hb, sc, whole(1...  6.18 us
    pallas_call x1, Pallas kernels, body(): heads_call(k_vgrad, [sc, sc, hb, hb, hb], hb, flat, big // 2, name='vgrad')  5.44 us
    all_to_all x3, waiting for transfers between devices, exchange(): return lax.all_to_all(x, axis, 0, 0, tiled=True, axis_index_groups=groups)  3.19 us
    pallas_call x1, Pallas kernels, body(): one_call(k_state, [work] * 4, vm, sds((G * PR, D)), 'state', big // 6, [p...  2.41 us
    pallas_call x1, Pallas kernels, body(): one_call(k_final, [vm] * 7, [work, work, vm], [pltpu.HBM((L, NH * D), BF1...  2.13 us
  transfers between devices with their start and end apart: 3, of which 3 were waited for; matrix products, arithmetic and copies ran while one was open for 0% of the time, Pallas kernels for 18%

profile of v3, /device:TPU:1, one launch (start us, length us, event | category | flops | bytes accessed | tf_op | source)
XLA Modules:
  0.0 104.4 jit_solution(2447213017571606558)
XLA Ops:
  0.6 2.4 %state.1 = f32[640,128]{1,0:T(8,128)S(1)} custom-call(s32[384]{0:T(512)} %seg_hbm.1, f32[4]{0:T(128)} %rate_ref.5, f32[384,512]{1,0:T(8,128)} %k_ref.7, f32[384,512]{1,0:T(8,128)} %v_ref.5), custom_call_target="tpu_custom_call" | custom-call | flops 226492416 | bytes 524288 | tf_op jit(solution)/shard_map/state/pallas_call | solution.py:437
  3.0 17.0 %all_to_all.77 = f32[16,40,128]{2,1,0:T(8,128)S(1)} all-to-all(f32[16,40,128]{2,1,0:T(8,128)S(1)} %bitcast.18), channel_id=1, replica_groups={{0,8,16,24,32,40,48,56,64,72,80,88,96,104,112,120},{128,136,144,152,160..., dimensions={0} | all-to-all | bytes 655360 | tf_op jit(solution)/shard_map/all_to_all | solution.py:414
  20.1 0.1 total.2
  20.1 14.1 %all_to_all.78 = f32[4,40,128]{2,1,0:T(8,128)S(1)} all-to-all(f32[4,40,128]{2,1,0:T(8,128)S(1)} %bitcast.24), channel_id=1, replica_groups={{0,128,256,384},{8,136,264,392},{16,144,272,400},{24,152,280,408},{32,1..., dimensions={0} | all-to-all | bytes 163840 | tf_op jit(solution)/shard_map/all_to_all | solution.py:414
  34.2 0.8 carry.2
  35.0 6.0 %all-to-all-start.2 = ((f32[16,32,128]{2,1,0:T(8,128)}), f32[16,32,128]{2,1,0:T(8,128)S(1)}, u32[]{:S(2)}, u32[]{:S(2)}) async-start(f32[16,32,128]{2,1,0:T(8,128)} %bitcast.4), calls=%async_computation.2 | async-start | bytes 524288 | tf_op jit(solution)/shard_map/all_to_all | solution.py:414
  41.0 0.0 copy-start
  41.0 0.0 copy-start.2
  41.0 6.2 %local.1 = (f32[384,512]{1,0:T(8,128)S(1)}, s32[8]{0:T(128)}, f32[16,128]{1,0:T(8,128)S(1)}) custom-call(s32[384]{0:T(512)} %seg_hbm.1, f32[4]{0:T(128)} %rate_ref.5, f32[384,512]{1,0:T(8,128)} %q_ref.9, f32[384,512]{1,0:T(8,128)} %k_ref.7, f32[384,512]{1,0:T(8,128)} %v_ref.5, f32[512]{0:T(512)} %gain_ref.1), custom_call_target="tpu_custom_call" | custom-call | flops 1358954496 | bytes 3145728 | tf_op jit(solution)/shard_map/local/pallas_call | solution.py:447
  47.2 1.1 %all-to-all-done.2 = f32[16,32,128]{2,1,0:T(8,128)S(1)} async-done(((f32[16,32,128]{2,1,0:T(8,128)}), f32[16,32,128]{2,1,0:T(8,128)S(1)}, u32[]{:S(2)}, u32[]{:S(2)}) %all-to-all-start.2) | async-done | bytes 262176 | tf_op jit(solution)/shard_map/all_to_all | solution.py:414
  48.2 0.0 copy-done
  48.2 0.0 copy-done.2
  48.2 0.8 norm.1
  49.0 13.5 %all_to_all.79 = f32[8,8,128]{2,1,0:T(8,128)S(1)} all-to-all(f32[8,8,128]{2,1,0:T(8,128)S(1)} %bitcast.27), channel_id=1, replica_groups=mesh['seq'=64,'head'=8] {'head'}, dimensions={0} | all-to-all | bytes 65536 | tf_op jit(solution)/shard_map/all_to_all | solution.py:414
  62.5 1.6 %grad.1 = (f32[384,512]{1,0:T(8,128)S(1)}, f32[640,128]{1,0:T(8,128)}) custom-call(f32[16,128]{1,0:T(8,128)S(1)} %get-tuple-element.19.con_ref, f32[64,128]{1,0:T(8,128)S(1)} %bitcast.26, f32[384,512]{1,0:T(8,128)S(1)} %copy-done.2, f32[384,512]{1,0:T(8,128)S(1)} %get-tuple-element.22.o_ref, f32[384,512]{1,0:T(8,128)S(1)} %copy-done), custom_call_target="tpu_custom_call" | custom-call | flops 226492416 | bytes 524288 | tf_op jit(solution)/shard_map/grad/pallas_call | solution.py:462
  64.1 0.0 copy-start.4
  64.1 6.2 %all-to-all-start.4 = ((f32[16,40,128]{2,1,0:T(8,128)}), f32[16,40,128]{2,1,0:T(8,128)S(1)}, u32[]{:S(2)}, u32[]{:S(2)}) async-start(f32[16,40,128]{2,1,0:T(8,128)} %bitcast.8), calls=%async_computation.4 | async-start | bytes 655360 | tf_op jit(solution)/shard_map/all_to_all | solution.py:414
  70.3 7.3 %pgrad.1 = (bf16[384,512]{1,0:T(8,128)(2,1)}, f32[384,512]{1,0:T(8,128)S(1)}) custom-call(s32[8]{0:T(128)} %get-tuple-element.18.bnd_ref, f32[4]{0:T(128)} %rate_ref.5, f32[384,512]{1,0:T(8,128)} %q_ref.9, f32[384,512]{1,0:T(8,128)} %k_ref.7, f32[384,512]{1,0:T(8,128)} %v_ref.5, f32[384,512]{1,0:T(8,128)S(1)} %get-tuple-element.23.do_ref, ...), custom_call_target="tpu_custom_call" | custom-call | flops 1358954496 | bytes 3145728 | tf_op jit(solution)/shard_map/pgrad/pallas_call | solution.py:471
  77.6 0.0 copy-done.4
  77.6 0.4 all-to-all-done.4
  78.0 0.1 total.3
  78.0 9.3 %all_to_all.80 = f32[4,40,128]{2,1,0:T(8,128)S(1)} all-to-all(f32[4,40,128]{2,1,0:T(8,128)S(1)} %bitcast.22), channel_id=1, replica_groups={{0,128,256,384},{8,136,264,392},{16,144,272,400},{24,152,280,408},{32,1..., dimensions={0} | all-to-all | bytes 163840 | tf_op jit(solution)/shard_map/all_to_all | solution.py:414
  87.4 0.8 carry.3
  88.1 6.9 %all-to-all-start.6 = ((f32[16,32,128]{2,1,0:T(8,128)}), f32[16,32,128]{2,1,0:T(8,128)S(1)}, u32[]{:S(2)}, u32[]{:S(2)}) async-start(f32[16,32,128]{2,1,0:T(8,128)} %bitcast.12), calls=%async_computation.6 | async-start | bytes 524288 | tf_op jit(solution)/shard_map/all_to_all | solution.py:414
  95.0 0.0 copy-start.1
  95.0 0.0 copy-start.3
  95.1 5.4 %vgrad.1.dvl_ref = f32[384,512]{1,0:T(8,128)S(1)} custom-call(s32[8]{0:T(128)} %get-tuple-element.18.bnd_ref, f32[4]{0:T(128)} %rate_ref.5, f32[384,512]{1,0:T(8,128)} %q_ref.9, f32[384,512]{1,0:T(8,128)} %k_ref.7, f32[384,512]{1,0:T(8,128)} %copy-done.4), custom_call_target="tpu_custom_call" | custom-call | flops 679477248 | bytes 3145728 | tf_op jit(solution)/shard_map/vgrad/pallas_call | solution.py:479
  100.5 1.7 %all-to-all-done.6 = f32[16,32,128]{2,1,0:T(8,128)S(1)} async-done(((f32[16,32,128]{2,1,0:T(8,128)}), f32[16,32,128]{2,1,0:T(8,128)S(1)}, u32[]{:S(2)}, u32[]{:S(2)}) %all-to-all-start.6) | async-done | bytes 262176 | tf_op jit(solution)/shard_map/all_to_all | solution.py:414
  102.2 0.0 copy-done.1
  102.2 0.0 copy-done.3
  102.2 2.1 %final.1 = (bf16[384,512]{1,0:T(8,128)(2,1)}, bf16[384,512]{1,0:T(8,128)(2,1)}, f32[512]{0:T(512)}) custom-call(f32[16,128]{1,0:T(8,128)S(1)} %get-tuple-element.19.con_ref, f32[384,512]{1,0:T(8,128)S(1)} %copy-done.1, f32[384,512]{1,0:T(8,128)S(1)} %copy-done.3, f32[512,128]{1,0:T(8,128)S(1)} %bitcast.21, f32[384,512]{1,0:T(8,128)S(1)} %get-tuple-element.26.rest_0_.dkl_ref, ...), custom_call_target="tpu_custom_call" | custom-call | flops 226492416 | bytes 524288 | tf_op jit(solution)/shard_map/final/pallas_call | solution.py:483
Async XLA Ops:
  35.0 13.3 %all-to-all-start.2 = ((f32[16,32,128]{2,1,0:T(8,128)}), f32[16,32,128]{2,1,0:T(8,128)S(1)}, u32[]{:S(2)}, u32[]{:S(2)}) async-start(f32[16,32,128]{2,1,0:T(8,128)} %bitcast.4), calls=%async_computation.2 | async-start | bytes 524288 | tf_op jit(solution)/shard_map/all_to_all | solution.py:414
  41.0 7.3 %copy-start = (f32[384,512]{1,0:T(8,128)S(1)}, f32[384,512]{1,0:T(8,128)}, u32[]{:S(2)}) copy-start(f32[384,512]{1,0:T(8,128)} %q_ref.9) | copy-start | bytes 2359300
  41.0 7.3 %copy-start.2 = (f32[384,512]{1,0:T(8,128)S(1)}, f32[384,512]{1,0:T(8,128)}, u32[]{:S(2)}) copy-start(f32[384,512]{1,0:T(8,128)} %og_ref.3) | copy-start | bytes 2359300
  64.1 13.5 %copy-start.4 = (f32[384,512]{1,0:T(8,128)}, f32[384,512]{1,0:T(8,128)S(1)}, u32[]{:S(2)}) copy-start(f32[384,512]{1,0:T(8,128)S(1)} %get-tuple-element.23.do_ref) | copy-start | bytes 2359300
  64.1 13.9 %all-to-all-start.4 = ((f32[16,40,128]{2,1,0:T(8,128)}), f32[16,40,128]{2,1,0:T(8,128)S(1)}, u32[]{:S(2)}, u32[]{:S(2)}) async-start(f32[16,40,128]{2,1,0:T(8,128)} %bitcast.8), calls=%async_computation.4 | async-start | bytes 655360 | tf_op jit(solution)/shard_map/all_to_all | solution.py:414
  88.1 14.1 %all-to-all-start.6 = ((f32[16,32,128]{2,1,0:T(8,128)}), f32[16,32,128]{2,1,0:T(8,128)S(1)}, u32[]{:S(2)}, u32[]{:S(2)}) async-start(f32[16,32,128]{2,1,0:T(8,128)} %bitcast.12), calls=%async_computation.6 | async-start | bytes 524288 | tf_op jit(solution)/shard_map/all_to_all | solution.py:414
  95.0 7.2 %copy-start.1 = (f32[384,512]{1,0:T(8,128)S(1)}, f32[384,512]{1,0:T(8,128)}, u32[]{:S(2)}) copy-start(f32[384,512]{1,0:T(8,128)} %k_ref.7) | copy-start | bytes 2359300
  95.0 7.2 %copy-start.3 = (f32[384,512]{1,0:T(8,128)S(1)}, f32[384,512]{1,0:T(8,128)}, u32[]{:S(2)}) copy-start(f32[384,512]{1,0:T(8,128)} %v_ref.5) | copy-start | bytes 2359300

commit v4 on v3

--- a/solution.py
+++ b/solution.py
@@ -273,7 +273,16 @@
         put_note(out_ref, h, notes(first, last, con_ref[h : h + 1, :], gains))
 
 
-def k_pgrad(bnd_ref, rate_ref, q_ref, k_ref, v_ref, do_ref, c_ref, dq_ref, dk_ref):
+def dot3k(a, b, ca, cb):
+    left = jnp.concatenate([a[0], a[1], a[0]], axis=ca)
+    right = jnp.concatenate([b[0], b[0], b[1]], axis=cb)
+    dims = (((ca,), (cb,)), ((), ()))
+    return lax.dot_general(left, right, dims, preferred_element_type=F32)
+
+
+def k_back(
+    bnd_ref, rate_ref, q_ref, k_ref, v_ref, do_ref, c_ref, after, dq_ref, both_ref
+):
     h = pl.program_id(0)
     rate = rate_ref[h]
     bounds = [bnd_ref[t] for t in range(5)]
@@ -282,40 +291,23 @@
     for rb in range(3):
         n = (rb + 1) * D
         rows = slice(rb * D, n)
-        dr = [x[rows] for x in ds]
-        p = split(dot3(dr, [x[:n] for x in vs], 1, 1) * weights(rate, bounds, rb))
+        qr, dr = [x[rows] for x in qs], [x[rows] for x in ds]
+        kc, vc = [x[:n] for x in ks], [x[:n] for x in vs]
+        w = weights(rate, bounds, rb)
+        p = split(dot3k(dr, vc, 1, 1) * w)
+        a = split(dot3k(qr, kc, 1, 1) * w)
         i = rows_iota(D) + rb * D
-        a = jnp.where(i < bnd_ref[5], jnp.exp(-rate * (i + 1).astype(F32)), 0.0)
-        dq = dot3(p, [x[:n] for x in ks], 1, 0) + a * dot3(dr, cs, 1, 1)
+        coef = jnp.where(i < bnd_ref[5], jnp.exp(-rate * (i + 1).astype(F32)), 0.0)
+        dq = dot3k(p, kc, 1, 0) + coef * dot3k(dr, cs, 1, 1)
         dq_ref[rows, :] = dq.astype(BF16)
-        part = dot3(p, [x[rows] for x in qs], 0, 0)
-        if rb == 0:
-            dk_ref[0:n, :] = part
-        else:
-            dk_ref[0 : n - D, :] += part[: n - D]
-            dk_ref[rows, :] = part[n - D :]
-
-
-def k_vgrad(bnd_ref, rate_ref, q_ref, k_ref, do_ref, dv_ref):
-    h = pl.program_id(0)
-    rate = rate_ref[h]
-    bounds = [bnd_ref[t] for t in range(5)]
-    qs, ks, ds = [split(x[...]) for x in (q_ref, k_ref, do_ref)]
-    for rb in range(3):
-        n = (rb + 1) * D
-        rows = slice(rb * D, n)
-        s = dot3([x[rows] for x in qs], [x[:n] for x in ks], 1, 1)
-        a = split(s * weights(rate, bounds, rb))
-        part = dot3(a, [x[rows] for x in ds], 0, 0)
-        if rb == 0:
-            dv_ref[0:n, :] = part
-        else:
-            dv_ref[0 : n - D, :] += part[: n - D]
-            dv_ref[rows, :] = part[n - D :]
+        for t, part in enumerate((dot3(p, qr, 0, 0), dot3(a, dr, 0, 0))):
+            if rb > 0:
+                both_ref[t, 0 : n - D, :] += part[: n - D]
+            both_ref[t, rows, :] = part[n - D :]
 
 
 def k_final(
-    con_ref, k_ref, v_ref, st_ref, dkl_ref, dvl_ref, gain_ref,
+    con_ref, k_ref, v_ref, st_ref, both_ref, gain_ref,
     dk_hbm, dv_hbm, gg_ref, dk_ref, dv_ref, sems,
 ):
     stores = []
@@ -326,8 +318,8 @@
         c = jnp.where(inside, jnp.exp(-con_ref[h : h + 1, :] * back), 0.0)
         ss = split(st_ref[head(h), :])
         gg_ref[head(h)] = gain_ref[GAIN + h, :]
-        dk = dkl_ref[:, head(h)] + c * dot3(split(v_ref[:, head(h)]), ss, 1, 1)
-        dv = dvl_ref[:, head(h)] + c * dot3(split(k_ref[:, head(h)]), ss, 1, 0)
+        dk = both_ref[0, :, head(h)] + c * dot3(split(v_ref[:, head(h)]), ss, 1, 1)
+        dv = both_ref[1, :, head(h)] + c * dot3(split(k_ref[:, head(h)]), ss, 1, 0)
         for t, (x, buf, out) in enumerate(((dk, dk_ref, dk_hbm), (dv, dv_ref, dv_hbm))):
             buf[:, head(h)] = x.astype(BF16)
             stores.append(
@@ -414,18 +406,18 @@
     return lax.all_to_all(x, axis, 0, 0, tiled=True, axis_index_groups=groups)
 
 
-def scan_groups(payload, reverse, order=()):
+def scan_groups(payload, reverse):
     vm = near_block()
     recv = exchange(payload)
     total = small_call(
-        functools.partial(k_total, reverse=reverse), 1, len(order), sds((NG * PR, D)), "total"
-    )(recv, *order)
+        functools.partial(k_total, reverse=reverse), 1, 0, sds((NG * PR, D)), "total"
+    )(recv)
     totals = exchange(total, "seq", COLUMNS)
     shapes = [sds((G * CH, D))] + ([pltpu.VMEM((8, D), F32)] if reverse else [])
     back, *gain = one_call(
         functools.partial(k_carry, reverse=reverse), [vm] * 2, [vm] * len(shapes), shapes, "carry"
     )(recv, totals)
-    return exchange(back), *near(*gain)
+    return exchange(back), *near(*gain), totals
 
 
 def body(queries, key_vectors, value_vectors, out_grad, norm_gain, decay_rates, segment_ids):
@@ -454,7 +446,7 @@
     )(segs, rates, q, k, v, *far(norm_gain))
     (bnd,) = far(bnd)
     (con,) = near(con)
-    (carry,) = scan_groups(payload, False)
+    carry, _ = scan_groups(payload, False)
     out, red = one_call(
         k_norm, [vm] * 5, [vm, vm], [flat, sds((64, D))], "norm", big // 6
     )(con, queries, carry, *near(local_out), out_grad)
@@ -468,27 +460,24 @@
         big // 6,
     )(con, sums, out_grad, *near(out), queries)
     (grad_out,) = near(grad_out)
-    dq, dk_local = heads_call(
-        k_pgrad,
-        [sc, sc, hb, hb, hb, hb, rows_block(D)],
-        [hb, hb],
-        [pltpu.HBM((L, NH * D), BF16), flat],
+    back, gain, totals = scan_groups(payload, True)
+    dq, both = heads_call(
+        k_back,
+        [sc, sc, hb, hb, hb, hb, rows_block(D), work],
+        [hb, pl.BlockSpec((2, L, D), lambda h: (0, 0, h))],
+        [pltpu.HBM((L, NH * D), BF16), pltpu.VMEM((2, L, NH * D), F32)],
         big,
-        name="pgrad",
-    )(bnd, rates, q, k, v, grad_out, carry)
-    dv_local = heads_call(
-        k_vgrad, [sc, sc, hb, hb, hb], hb, flat, big // 2, name="vgrad"
-    )(bnd, rates, q, k, *far(grad_out))
-    back, gain = scan_groups(payload, True, (dk_local,))
+        name="back",
+    )(bnd, rates, q, k, v, *far(grad_out), carry, totals)
     dk, dv, gain_grad = one_call(
         k_final,
-        [vm] * 7,
+        [vm] * 6,
         [work, work, vm],
         [pltpu.HBM((L, NH * D), BF16)] * 2 + [sds((NH * D,))],
         "final",
         big // 6,
         [pltpu.VMEM((L, NH * D), BF16)] * 2 + [pltpu.SemaphoreType.DMA((2 * NH,))],
-    )(con, key_vectors, value_vectors, back, *near(dk_local, dv_local), gain)
+    )(con, key_vectors, value_vectors, back, *near(both), gain)
     return dq, dk, dv, gain_grad
 
 

time: 105 us -> 105 us (level)
  blocking collectives: 53.9 us -> 67.6 us
  starting transfers between devices: 19.1 us -> 12.4 us
  Pallas kernels: 27.5 us -> 22.4 us
  waiting for transfers between devices: 3.19 us -> 1.06 us
    all_to_all x4 -> x5, blocking collectives: 53.9 us -> 67.6 us  [exchange(): return lax.all_to_all(x, axis, 0, 0, tiled=True, axis_index_groups=groups)]
    all_to_all x3 -> x2, starting transfers between devices: 19.1 us -> 12.4 us  [exchange(): return lax.all_to_all(x, axis, 0, 0, tiled=True, axis_index_groups=groups)]
    pallas_call x5 -> x4, Pallas kernels: 15 us -> 10.7 us  [the longest x1 7.47 us: body(): heads_call(k_back, [sc, sc, hb, hb, hb, hb, rows_block(D), work], [hb, pl...]
    all_to_all x3 -> x2, waiting for transfers between devices: 3.19 us -> 1.06 us  [exchange(): return lax.all_to_all(x, axis, 0, 0, tiled=True, axis_index_groups=groups)]
  transfers between devices with their start and end apart: 3 -> 2, of which waited for: 3 -> 1; matrix products, arithmetic and copies ran while one was open for 0% -> 0% of each run, Pallas kernels for 18% -> 13%
where the time goes in v4:
time: 105 us; the launch traced here: 104 us
  blocking collectives  67.6 us (64%)
  Pallas kernels  22.4 us (21%)
  starting transfers between devices  12.4 us (12%)
  waiting for transfers between devices  1.06 us (1%)
    all_to_all x5, blocking collectives, exchange(): return lax.all_to_all(x, axis, 0, 0, tiled=True, axis_index_groups=groups)  67.6 us
    all_to_all x2, starting transfers between devices, exchange(): return lax.all_to_all(x, axis, 0, 0, tiled=True, axis_index_groups=groups)  12.4 us
    pallas_call x1, Pallas kernels, body(): heads_call(k_back, [sc, sc, hb, hb, hb, hb, rows_block(D), work], [hb, pl...  7.47 us
    pallas_call x1, Pallas kernels, body(): heads_call(k_local, [sc, sc, hb, hb, hb, whole(NH * D)], [hb, sc, whole(1...  6.18 us
    pallas_call x1, Pallas kernels, body(): one_call(k_final, [vm] * 6, [work, work, vm], [pltpu.HBM((L, NH * D), BF1...  3.09 us
    pallas_call x1, Pallas kernels, body(): one_call(k_state, [work] * 4, vm, sds((G * PR, D)), 'state', big // 6, [p...  2.41 us
  transfers between devices with their start and end apart: 2, of which 1 were waited for; matrix products, arithmetic and copies ran while one was open for 0% of the time, Pallas kernels for 13%

profile of v4, /device:TPU:1, one launch (start us, length us, event | category | flops | bytes accessed | tf_op | source)
XLA Modules:
  0.0 104.3 jit_solution(11381844884076451353)
XLA Ops:
  0.6 2.4 %state.1 = f32[640,128]{1,0:T(8,128)S(1)} custom-call(s32[384]{0:T(512)} %seg_hbm.1, f32[4]{0:T(128)} %rate_ref.3, f32[384,512]{1,0:T(8,128)} %k_ref.5, f32[384,512]{1,0:T(8,128)} %v_ref.5), custom_call_target="tpu_custom_call" | custom-call | flops 226492416 | bytes 524288 | tf_op jit(solution)/shard_map/state/pallas_call | solution.py:429
  3.0 17.0 %all_to_all.77 = f32[16,40,128]{2,1,0:T(8,128)S(1)} all-to-all(f32[16,40,128]{2,1,0:T(8,128)S(1)} %bitcast.18), channel_id=1, replica_groups={{0,8,16,24,32,40,48,56,64,72,80,88,96,104,112,120},{128,136,144,152,160..., dimensions={0} | all-to-all | bytes 655360 | tf_op jit(solution)/shard_map/all_to_all | solution.py:406
  20.1 0.1 total.2
  20.1 14.1 %all_to_all.78 = f32[4,40,128]{2,1,0:T(8,128)S(1)} all-to-all(f32[4,40,128]{2,1,0:T(8,128)S(1)} %bitcast.24), channel_id=1, replica_groups={{0,128,256,384},{8,136,264,392},{16,144,272,400},{24,152,280,408},{32,1..., dimensions={0} | all-to-all | bytes 163840 | tf_op jit(solution)/shard_map/all_to_all | solution.py:406
  34.2 0.8 carry.2
  35.0 6.0 %all-to-all-start.2 = ((f32[16,32,128]{2,1,0:T(8,128)}), f32[16,32,128]{2,1,0:T(8,128)S(1)}, u32[]{:S(2)}, u32[]{:S(2)}) async-start(f32[16,32,128]{2,1,0:T(8,128)} %bitcast.4), calls=%async_computation.2 | async-start | bytes 524288 | tf_op jit(solution)/shard_map/all_to_all | solution.py:406
  41.0 0.0 copy-start
  41.0 0.0 copy-start.1
  41.0 6.2 %local.1 = (f32[384,512]{1,0:T(8,128)S(1)}, s32[8]{0:T(128)}, f32[16,128]{1,0:T(8,128)S(1)}) custom-call(s32[384]{0:T(512)} %seg_hbm.1, f32[4]{0:T(128)} %rate_ref.3, f32[384,512]{1,0:T(8,128)} %q_ref.7, f32[384,512]{1,0:T(8,128)} %k_ref.5, f32[384,512]{1,0:T(8,128)} %v_ref.5, f32[512]{0:T(512)} %gain_ref.1), custom_call_target="tpu_custom_call" | custom-call | flops 1358954496 | bytes 3145728 | tf_op jit(solution)/shard_map/local/pallas_call | solution.py:439
  47.2 1.1 %all-to-all-done.2 = f32[16,32,128]{2,1,0:T(8,128)S(1)} async-done(((f32[16,32,128]{2,1,0:T(8,128)}), f32[16,32,128]{2,1,0:T(8,128)S(1)}, u32[]{:S(2)}, u32[]{:S(2)}) %all-to-all-start.2) | async-done | bytes 262176 | tf_op jit(solution)/shard_map/all_to_all | solution.py:406
  48.2 0.0 copy-done
  48.2 0.0 copy-done.1
  48.2 0.8 norm.1
  49.0 13.5 %all_to_all.79 = f32[8,8,128]{2,1,0:T(8,128)S(1)} all-to-all(f32[8,8,128]{2,1,0:T(8,128)S(1)} %bitcast.28), channel_id=1, replica_groups=mesh['seq'=64,'head'=8] {'head'}, dimensions={0} | all-to-all | bytes 65536 | tf_op jit(solution)/shard_map/all_to_all | solution.py:406
  62.5 0.9 grad.1
  63.4 0.0 copy-start.4
  63.4 13.7 %all_to_all.80 = f32[16,40,128]{2,1,0:T(8,128)S(1)} all-to-all(f32[16,40,128]{2,1,0:T(8,128)S(1)} %bitcast.21), channel_id=1, replica_groups={{0,8,16,24,32,40,48,56,64,72,80,88,96,104,112,120},{128,136,144,152,160..., dimensions={0} | all-to-all | bytes 655360 | tf_op jit(solution)/shard_map/all_to_all | solution.py:406
  77.1 0.1 total.3
  77.1 9.3 %all_to_all.81 = f32[4,40,128]{2,1,0:T(8,128)S(1)} all-to-all(f32[4,40,128]{2,1,0:T(8,128)S(1)} %bitcast.25), channel_id=1, replica_groups={{0,128,256,384},{8,136,264,392},{16,144,272,400},{24,152,280,408},{32,1..., dimensions={0} | all-to-all | bytes 163840 | tf_op jit(solution)/shard_map/all_to_all | solution.py:406
  86.5 0.8 carry.3
  87.2 6.4 %all-to-all-start.6 = ((f32[16,32,128]{2,1,0:T(8,128)}), f32[16,32,128]{2,1,0:T(8,128)}, u32[]{:S(2)}, u32[]{:S(2)}) async-start(f32[16,32,128]{2,1,0:T(8,128)} %bitcast.12), calls=%async_computation.6 | async-start | bytes 524288 | tf_op jit(solution)/shard_map/all_to_all | solution.py:406
  93.7 0.0 copy-done.4
  93.7 0.0 copy-start.2
  93.7 0.0 copy-start.3
  93.7 7.5 %back.1 = (bf16[384,512]{1,0:T(8,128)(2,1)}, f32[2,384,512]{2,1,0:T(8,128)S(1)}) custom-call(s32[8]{0:T(128)} %get-tuple-element.18.bnd_ref, f32[4]{0:T(128)} %rate_ref.3, f32[384,512]{1,0:T(8,128)} %q_ref.7, f32[384,512]{1,0:T(8,128)} %k_ref.5, f32[384,512]{1,0:T(8,128)} %v_ref.5, f32[384,512]{1,0:T(8,128)} %copy-done.4, f32[512,128]{1,0:T(8,128)S(1)} %bitcast.20, ...), custom_call_target="tpu_custom_call" | custom-call | flops 1358954496 | bytes 3145728 | tf_op jit(solution)/shard_map/back/pallas_call | solution.py:464
  101.2 0.0 all-to-all-done.6
  101.2 0.0 copy-done.2
  101.2 0.0 copy-done.3
  101.2 3.1 %final.1 = (bf16[384,512]{1,0:T(8,128)(2,1)}, bf16[384,512]{1,0:T(8,128)(2,1)}, f32[512]{0:T(512)}) custom-call(f32[16,128]{1,0:T(8,128)S(1)} %get-tuple-element.19.con_ref, f32[384,512]{1,0:T(8,128)S(1)} %copy-done.2, f32[384,512]{1,0:T(8,128)S(1)} %copy-done.3, f32[512,128]{1,0:T(8,128)} %bitcast.13.st_ref, f32[2,384,512]{2,1,0:T(8,128)S(1)} %get-tuple-element.27.both_ref, ...), custom_call_target="tpu_custom_call" | custom-call | flops 226492416 | bytes 524288 | tf_op jit(solution)/shard_map/final/pallas_call | solution.py:472
Async XLA Ops:
  35.0 13.3 %all-to-all-start.2 = ((f32[16,32,128]{2,1,0:T(8,128)}), f32[16,32,128]{2,1,0:T(8,128)S(1)}, u32[]{:S(2)}, u32[]{:S(2)}) async-start(f32[16,32,128]{2,1,0:T(8,128)} %bitcast.4), calls=%async_computation.2 | async-start | bytes 524288 | tf_op jit(solution)/shard_map/all_to_all | solution.py:406
  41.0 7.3 %copy-start = (f32[384,512]{1,0:T(8,128)S(1)}, f32[384,512]{1,0:T(8,128)}, u32[]{:S(2)}) copy-start(f32[384,512]{1,0:T(8,128)} %og_ref.3) | copy-start | bytes 2359300
  41.0 7.3 %copy-start.1 = (f32[384,512]{1,0:T(8,128)S(1)}, f32[384,512]{1,0:T(8,128)}, u32[]{:S(2)}) copy-start(f32[384,512]{1,0:T(8,128)} %q_ref.7) | copy-start | bytes 2359300
  63.4 30.3 %copy-start.4 = (f32[384,512]{1,0:T(8,128)}, f32[384,512]{1,0:T(8,128)S(1)}, u32[]{:S(2)}) copy-start(f32[384,512]{1,0:T(8,128)S(1)} %get-tuple-element.23.do_ref) | copy-start | bytes 2359300
  87.2 13.9 %all-to-all-start.6 = ((f32[16,32,128]{2,1,0:T(8,128)}), f32[16,32,128]{2,1,0:T(8,128)}, u32[]{:S(2)}, u32[]{:S(2)}) async-start(f32[16,32,128]{2,1,0:T(8,128)} %bitcast.12), calls=%async_computation.6 | async-start | bytes 524288 | tf_op jit(solution)/shard_map/all_to_all | solution.py:406
  93.7 7.5 %copy-start.2 = (f32[384,512]{1,0:T(8,128)S(1)}, f32[384,512]{1,0:T(8,128)}, u32[]{:S(2)}) copy-start(f32[384,512]{1,0:T(8,128)} %k_ref.5) | copy-start | bytes 2359300
  93.7 7.5 %copy-start.3 = (f32[384,512]{1,0:T(8,128)S(1)}, f32[384,512]{1,0:T(8,128)}, u32[]{:S(2)}) copy-start(f32[384,512]{1,0:T(8,128)} %v_ref.5) | copy-start | bytes 2359300
